TPU v7x, 32 devices: a whole 2x2x4 slice. The times are simulated.
32 devices in a mesh: grp: 2 (over y), rx: 4 (over z), tw: 2 (over x), fq: 2 (over core).
Axes of the slice: x: 2, y: 2, z: 4, core: 2. Of those that a mesh axis runs over, the one named last changes fastest.
Arguments:
- traces: bfloat16 [8, 256, 15360], P('tw', ('grp', 'rx')), parts along dimension 1, may hold values from -48 to 48
- src_index: int32 [8, 64], P('grp'), parts along dimension 0, may hold values from 0 to 127
- valid: int32 [8, 256], P(None, 'grp'), parts along dimension 1, may hold values from 0 to 1, as said below
Outputs:
- correlations: bfloat16 [256, 256, 512], P(('tw', 'fq'), ('grp', 'rx')), parts along dimension 1
There are 2 independent parts, one for each index of `grp`. A program takes and returns all parts, laid end to end along the dimension named above; each array names one. Nothing has to cross between parts.
Inputs may be any that keep to these rules, and one draw needn't show every extreme that they name: `valid`: some channels may be 0 in every window, and some windows 0 on every channel. `src_index`: A channel may be named by several sources.
All inputs are finite; a program needn't handle non-finite values.
Results may differ from a plain program's by a relative error of at most 0.0062.
Values may be sent and summed in bfloat16 or wider, within the bound.
No kernel may reach another device: no remote copies, remote signals or barrier semaphores. Data moves between devices by JAX's collectives and lax.ppermute only.
A program may use at most 128 MiB of HBM per device.

v0:
```python
import math

import jax
import jax.numpy as jnp
from jax import lax
from jax.sharding import PartitionSpec as P

NT = 15360
BAND = 512
F0 = 60
HW = 32
LAGS = 512


two_pi = 2.0 * math.pi
eps_power = 1e-05


def padded_2(block, sides, width):
    for axis, dim in sides:
        count = lax.axis_size(axis)
        forward = [(i, i + 1) for i in range(count - 1)]
        backward = [(target, source) for source, target in forward]
        low = lax.ppermute(
            lax.slice_in_dim(block, block.shape[dim] - width, None, axis=dim), axis, forward
        )
        high = lax.ppermute(lax.slice_in_dim(block, 0, width, axis=dim), axis, backward)
        block = jnp.concatenate([low, block, high], axis=dim)
    return block


def forward_block(row_count, bin_ids, period):
    sample_ids = lax.broadcasted_iota(jnp.int32, (row_count, 1, 1), 0)
    phase_index = sample_ids * bin_ids[None, :, :] % period
    angle_rad = phase_index.astype(jnp.float32) * (two_pi / period)
    coef_block = jnp.stack([jnp.cos(angle_rad), -jnp.sin(angle_rad)], axis=2)
    return coef_block.reshape(row_count, -1).astype(jnp.bfloat16)


def inverse_rows(bin_ids, lag_count, period):
    lag_shift = lax.broadcasted_iota(jnp.int32, (1, lag_count), 1) - lag_count // 2
    phase_index = bin_ids[..., None] * lag_shift % period
    angle_rad = phase_index.astype(jnp.float32) * (two_pi / period)
    return jnp.concatenate([jnp.cos(angle_rad), -jnp.sin(angle_rad)], axis=-2).astype(jnp.bfloat16)


def shards(traces, src_index, valid):
    win_count, chan_count, samples = traces.shape
    tw_count = lax.axis_size("tw")
    fq_count = lax.axis_size("fq")
    tw_pos = lax.axis_index("tw")
    fq_pos = lax.axis_index("fq")
    rx_pos = lax.axis_index("rx")
    band_share = BAND // fq_count
    narrow = band_share // tw_count
    block_len = 1024
    trace_rows = traces.reshape(win_count * chan_count, samples)
    local_bins = (
        F0
        + fq_pos * band_share
        + lax.broadcasted_iota(jnp.int32, (tw_count, narrow), 0) * narrow
        + lax.broadcasted_iota(jnp.int32, (tw_count, narrow), 1)
    )
    base_table = forward_block(block_len, local_bins, samples)

    def accumulate(turn_index, running):
        offset = turn_index * block_len
        trace_piece = lax.dynamic_slice_in_dim(trace_rows, offset, block_len, 1)
        partial_value = jnp.dot(trace_piece, base_table, preferred_element_type=jnp.float32)
        partial_value = partial_value.reshape(-1, tw_count, 2, narrow)
        part_real = partial_value[:, :, 0]
        part_imag = partial_value[:, :, 1]
        phase_index = offset * local_bins % samples
        angle_rad = phase_index.astype(jnp.float32) * (two_pi / samples)
        turn_real = jnp.cos(angle_rad)[None]
        turn_imag = -jnp.sin(angle_rad)[None]
        new_real = part_real * turn_real - part_imag * turn_imag
        new_imag = part_real * turn_imag + part_imag * turn_real
        return running + jnp.stack([new_real, new_imag], axis=2)

    spec_parts = lax.fori_loop(
        0,
        samples // block_len,
        accumulate,
        jnp.zeros((win_count * chan_count, tw_count, 2, narrow), jnp.float32),
    )
    bin_power = (
        spec_parts[:, :, 0] * spec_parts[:, :, 0] + spec_parts[:, :, 1] * spec_parts[:, :, 1]
    )
    bin_power = bin_power.reshape(-1, band_share)
    padded = padded_2(bin_power, (("fq", 1),), HW)
    row_ids = lax.broadcasted_iota(jnp.int32, (band_share + 2 * HW, band_share), 0)
    col_ids = lax.broadcasted_iota(jnp.int32, (band_share + 2 * HW, band_share), 1)
    box_matrix = ((row_ids - col_ids >= 0) & (row_ids - col_ids <= 2 * HW)).astype(jnp.float32)
    smooth = jnp.dot(
        padded, box_matrix, precision=lax.Precision.HIGHEST, preferred_element_type=jnp.float32
    ) / (2 * HW + 1)
    white_gain = lax.rsqrt(smooth + eps_power).reshape(-1, tw_count, 1, narrow)
    whitened = (
        (spec_parts * white_gain)
        .astype(jnp.bfloat16)
        .reshape(win_count, chan_count, tw_count, 2 * narrow)
    )
    valid_float = valid.astype(jnp.float32)
    source_ids = src_index.reshape(-1)
    src_total = source_ids.shape[0]
    channels_all = valid.shape[1]
    pick_all = (
        lax.broadcasted_iota(jnp.int32, (channels_all, src_total), 0) == source_ids[None, :]
    ).astype(jnp.float32)
    source_valid = jnp.dot(
        valid_float, pick_all, precision=lax.Precision.HIGHEST, preferred_element_type=jnp.float32
    )
    receiver_valid = lax.dynamic_slice_in_dim(valid_float, rx_pos * chan_count, chan_count, 1)
    pair_count = jnp.dot(
        source_valid.T,
        receiver_valid,
        precision=lax.Precision.HIGHEST,
        preferred_element_type=jnp.float32,
    )
    pair_floor = jnp.maximum(pair_count, 1.0)[:, :, None]
    pick_local = (
        source_ids[:, None]
        == rx_pos * chan_count + lax.broadcasted_iota(jnp.int32, (1, chan_count), 1)
    ).astype(jnp.bfloat16)
    inv_scale = 1.0 / math.sqrt(BAND)
    own_block = tw_pos * fq_count + fq_pos
    src_local = src_total // (tw_count * fq_count)
    local_terms = jnp.einsum(
        "sc,wcx->swx",
        pick_local,
        whitened.reshape(win_count, chan_count, tw_count * 2 * narrow),
        preferred_element_type=jnp.float32,
    )
    sources = lax.psum(local_terms.astype(jnp.bfloat16), "rx")
    own_sources = lax.all_to_all(
        sources[None], ("tw", "fq"), split_axis=1, concat_axis=0, tiled=True
    )
    all_windows = lax.all_gather(whitened[None], ("tw", "fq"), axis=0, tiled=True)
    src_valid_own = lax.dynamic_slice_in_dim(source_valid, own_block * src_local, src_local, 1)
    src_valid_own = jnp.transpose(src_valid_own.reshape(tw_count, win_count, src_local), (0, 2, 1))
    own_sources = own_sources.reshape(
        tw_count, fq_count, src_local, win_count, tw_count, 2, narrow
    ) * src_valid_own.reshape(tw_count, 1, src_local, win_count, 1, 1, 1).astype(jnp.bfloat16)
    all_windows = all_windows.reshape(
        tw_count, fq_count, win_count, chan_count, tw_count, 2, narrow
    ) * receiver_valid.reshape(tw_count, 1, win_count, chan_count, 1, 1, 1).astype(jnp.bfloat16)
    src_real = own_sources[..., 0, :]
    src_imag = own_sources[..., 1, :]
    rec_real = all_windows[..., 0, :]
    rec_imag = all_windows[..., 1, :]
    pattern = "tfswbx,tfwcbx->scfbx"
    cross_real = jnp.einsum(
        pattern, src_real, rec_real, preferred_element_type=jnp.float32
    ) + jnp.einsum(pattern, src_imag, rec_imag, preferred_element_type=jnp.float32)
    cross_imag = jnp.einsum(
        pattern, src_real, rec_imag, preferred_element_type=jnp.float32
    ) - jnp.einsum(pattern, src_imag, rec_real, preferred_element_type=jnp.float32)
    floor_own = lax.dynamic_slice_in_dim(pair_floor, own_block * src_local, src_local, 0)
    stacked = jnp.concatenate(
        [
            cross_real.reshape(src_local, chan_count, BAND),
            cross_imag.reshape(src_local, chan_count, BAND),
        ],
        axis=2,
    )
    stacked = (stacked / floor_own).astype(jnp.bfloat16)
    inv_table = inverse_rows(F0 + lax.broadcasted_iota(jnp.int32, (BAND,), 0), LAGS, NT)
    summed = jnp.dot(
        stacked.reshape(src_local * chan_count, 2 * BAND),
        inv_table,
        preferred_element_type=jnp.float32,
    ).reshape(src_local, chan_count, LAGS)
    return (summed * inv_scale).astype(jnp.bfloat16)


def solution(mesh):
    return jax.shard_map(
        shards,
        mesh=mesh,
        in_specs=(P("tw", ("grp", "rx"), None), P("grp", None), P(None, "grp")),
        out_specs=P(("tw", "fq"), ("grp", "rx"), None),
        check_vma=False,
    )
```

profile of v0, /device:TPU:0, one launch (start us, length us, event | category | flops | bytes accessed | tf_op | source)
XLA Modules:
  0.0 195.9 jit_solution(17614216192900421187)
XLA Ops:
  6.6 4.6 %cosine_convert_fusion.1 = (bf16[1024,2,1,128]{3,0,2,1:T(8,128)(2,1)S(1)}, bf16[1024,2,1,128]{3,0,2,1:T(8,128)(2,1)S(1)}) fusion(s32[2,128]{1,0:T(2,128)S(1)} %iota_add_fusion.2), kind=kLoop, calls=%fused_computation.47 | loop fusion | flops 3145728 | bytes 1049600 | tf_op jit(solution)/shard_map/convert.2
  11.3 0.5 copy.35
  11.8 0.5 copy.36
  12.4 34.7 %while.16 = (s32[]{:T(128)}, f32[128,2,2,128]{3,2,1,0:T(2,128)S(1)}, bf16[128,15360]{1,0:T(8,128)(2,1)}, bf16[1024,512]{1,0:T(8,128)(2,1)S(1)}, s32[2]{0:T(128)S...) while((s32[]{:T(128)}, f32[128,2,2,128]{3,2,1,0:T(2,128)S(1)}, ...), condition=%wide.region_1.2_spmd.clone, body=%wide.region_0.1_spmd.clone.sunk | while | flops 134613760 | bytes 3412133 | solution.py:81
  12.4 1.3 fusion.68
  14.3 0.4 maximum_add_fusion.2
  14.7 1.3 fusion.68
  16.6 0.4 maximum_add_fusion.2
  17.1 1.3 fusion.68
  18.9 0.4 maximum_add_fusion.2
  19.4 1.3 fusion.68
  21.2 0.4 maximum_add_fusion.2
  21.7 1.3 fusion.68
  23.5 0.4 maximum_add_fusion.2
  24.0 1.3 fusion.68
  25.9 0.4 maximum_add_fusion.2
  26.3 1.3 fusion.68
  28.2 0.4 maximum_add_fusion.2
  28.6 1.3 fusion.68
  31.0 1.3 fusion.68
  33.3 1.3 fusion.68
  35.6 1.3 fusion.68
  37.9 1.3 fusion.68
  40.2 1.3 fusion.68
  42.5 1.3 fusion.68
  44.8 1.3 fusion.68
  47.1 0.5 add_reduce_fusion
  47.8 2.4 %collective-permute-start = (f32[128,32]{1,0:T(8,128)S(1)}, f32[128,32]{1,0:T(8,128)S(1)}, u32[]{:S(2)}, u32[]{:S(2)}) collective-permute-start(f32[128,32]{1,0:T(8,128)S(1)} %get-tuple-element.179), channel_id=1, source_target_pairs={{0,1},{2,3},{4,5},{6,7},{8,9},{10,11},{12,13},{14,15},{16,17},{18,... | collective-permute-start | bytes 49160 | tf_op jit(solution)/shard_map/ppermute | solution.py:24
  50.2 1.3 collective-permute-start.1
  51.6 1.7 collective-permute-done.1
  54.0 1.5 fusion.14
  56.1 53.5 %all-reduce.2.cloned.1.call-done = bf16[1,256,4,512]{3,1,2,0:T(8,128)(2,1)} async-done(((bf16[1,256,4,512]{3,1,2,0:T(8,128)(2,1)}), bf16[1,256,4,512]{3,1,2,0:T(8,128)(2,1)}) %all-reduce.2.cloned.1.call-update) | async-done | bytes 1048592 | tf_op jit(solution)/shard_map/psum | solution.py:135
  109.7 3.0 %copy.40 = bf16[1,256,4,512]{3,2,0,1:T(4,128)(2,1)} copy(bf16[1,256,4,512]{3,1,2,0:T(8,128)(2,1)} %all-reduce.2.cloned.1.call-done) | data formatting | bytes 2097152 | tf_op jit(solution)/shard_map/psum | solution.py:135
  112.7 4.3 %all-to-all-start = ((bf16[1,256,4,512]{3,2,0,1:T(4,128)(2,1)}), bf16[1,256,4,512]{3,2,0,1:T(4,128)(2,1)}, u32[]{:S(2)}, u32[]{:S(2)}) async-start(bf16[1,256,4,512]{3,2,0,1:T(4,128)(2,1)} %copy.40), calls=%async_computation | async-start | bytes 2097152 | tf_op jit(solution)/shard_map/all_to_all | solution.py:136
  117.1 5.7 %cosine_convert_fusion = (bf16[512,512]{1,0:T(8,128)(2,1)}, bf16[512,512]{1,0:T(8,128)(2,1)}) fusion(s32[512]{0:T(512)S(1)} %get-tuple-element.185, s32[512]{0:T(512)S(1)} %get-tuple-element.186), kind=kLoop, calls=%fused_computation.40 | loop fusion | flops 3145728 | bytes 1052672 | tf_op jit(solution)/shard_map/convert
  123.0 12.0 %all_gather.3 = bf16[4,4,32,2,256]{4,2,3,1,0:T(8,128)(2,1)S(1)} all-gather(bf16[1,4,32,2,256]{4,2,3,1,0:T(8,128)(2,1)S(1)} %copy.38), channel_id=1, replica_groups=mesh['grp'=2,'rx'=4,'tw'=2,'fq'=2] {'tw','fq'}, dimensions={0}, use_global_device_ids=true | all-gather | bytes 655360 | tf_op jit(solution)/shard_map/all_gather | solution.py:139
  135.1 2.5 %copy.39 = bf16[2,2,4,32,2,2,128]{3,2,0,6,4,1,5:T(4,128)(2,1)} copy(bf16[2,2,4,32,2,2,128]{6,5,3,4,2,1,0:T(2,128)(2,1)S(1)} %reshape.161) | data formatting | bytes 1048576 | tf_op jit(solution)/shard_map/reshape | solution.py:145
  137.7 1.7 broadcast_multiply_fusion.1
  139.4 1.5 reshape.171
  140.9 4.3 %copy.42 = bf16[2,2,64,4,2,2,128]{2,3,0,6,4,1,5:T(4,128)(2,1)} copy(bf16[2,2,64,4,2,2,128]{6,5,4,3,2,1,0:T(2,128)(2,1)S(1)} %reshape.171) | data formatting | bytes 2097152 | tf_op jit(solution)/shard_map/reshape | solution.py:142
  145.1 1.7 broadcast_multiply_fusion
  146.9 1.8 fusion.29
  148.7 4.2 %fusion.30 = f32[2,2,128,32,64,1]{4,3,5,2,1,0:T(8,128)} fusion(bf16[2,2,64,4,2,2,128]{2,3,0,6,4,1,5:T(4,128)(2,1)S(1)} %bitcast.78, bf16[2,2,4,32,2,2,128]{3,2,0,6,4,1,5:T(4,128)(2,1)S(1)} %bitcast.74), kind=kOutput, calls=%fused_computation.54 | convolution fusion | flops 16777216 | bytes 6291456 | tf_op jit(solution)/shard_map/tfswbx,tfwcbx->scfbx/dot_general | solution.py:156
  152.9 4.3 %bitcast_add_fusion = f32[2,2,128,32,64]{4,3,2,1,0:T(8,128)} fusion(f32[2,2,128,32,64,1]{4,3,5,2,1,0:T(8,128)S(1)} %fusion.29, bf16[2,2,4,32,2,2,128]{3,2,0,6,4,1,5:T(4,128)(2,1)S(1)} %bitcast.75, bf16[2,2,64,4,2,2,128]{2,3,0,6,4,1,5:T(4,128)(2,1)S(1)} %bitcast.79), kind=kOutput, calls=%fused_computation.17 | convolution fusion | flops 17825792 | bytes 14680064 | tf_op jit(solution)/shard_map/tfswbx,tfwcbx->scfbx/dot_general | solution.py:155
  157.2 7.7 %copy.43 = f32[64,32,512]{2,1,0:T(8,128)} copy(f32[64,32,512]{0,1,2:T(8,128)} %bitcast.72) | data formatting | bytes 8388608 | tf_op jit(solution)/shard_map/concatenate | solution.py:160
  165.0 9.1 %bitcast_subtract_fusion = f32[2,2,128,32,64]{4,3,2,1,0:T(8,128)} fusion(f32[2,2,128,32,64,1]{4,3,5,2,1,0:T(8,128)} %fusion.30, bf16[2,2,4,32,2,2,128]{3,2,0,6,4,1,5:T(4,128)(2,1)S(1)} %bitcast.76, bf16[2,2,64,4,2,2,128]{2,3,0,6,4,1,5:T(4,128)(2,1)} %bitcast.80), kind=kOutput, calls=%fused_computation.16 | convolution fusion | flops 17825792 | bytes 14680064 | tf_op jit(solution)/shard_map/tfswbx,tfwcbx->scfbx/dot_general | solution.py:158
  174.0 7.8 %copy.44 = f32[64,32,512]{2,1,0:T(8,128)} copy(f32[64,32,512]{0,1,2:T(8,128)} %bitcast.71) | data formatting | bytes 8388608 | tf_op jit(solution)/shard_map/concatenate | solution.py:160
  181.8 7.2 %multiply_convert_fusion = bf16[64,32,512]{2,1,0:T(8,128)(2,1)} fusion(f32[64,32,512]{2,1,0:T(8,128)} %copy.44, f32[64,32,512]{2,1,0:T(8,128)} %copy.43, f32[64,32]{1,0:T(8,128)S(1)} %copy.45, bf16[512,512]{1,0:T(8,128)(2,1)S(1)} %copy-done.2, bf16[512,512]{1,0:T(8,128)(2,1)S(1)} %copy-done.1), kind=kOutput, calls=%fused_computation.18 | convolution fusion | flops 2157969408 | bytes 11542528 | tf_op jit(solution)/shard_map/dot_general | solution.py:169
  (90 shorter events, 14.1 us)
Async XLA Ops:
  6.5 103.1 %all-reduce.2.cloned.1.call-start = ((), (), s32[]{:S(2)}) async-start(), calls=%async_computation.1 | async-start | bytes 2097152 | tf_op jit(solution)/shard_map/psum | solution.py:135
  12.4 39.1 %copy-start.4 = (s32[4,64]{1,0:T(4,128)S(1)}, s32[4,64]{1,0:T(4,128)}, u32[]{:S(2)}) copy-start(s32[4,64]{1,0:T(4,128)} %param.6) | copy-start | bytes 3076
  47.7 7.8 %copy-start.3 = (s32[8,128]{1,0:T(8,128)S(1)}, s32[8,128]{1,0:T(8,128)}, u32[]{:S(2)}) copy-start(s32[8,128]{1,0:T(8,128)} %param.7) | copy-start | bytes 12292
  47.8 3.8 %collective-permute-start = (f32[128,32]{1,0:T(8,128)S(1)}, f32[128,32]{1,0:T(8,128)S(1)}, u32[]{:S(2)}, u32[]{:S(2)}) collective-permute-start(f32[128,32]{1,0:T(8,128)S(1)} %get-tuple-element.179), channel_id=1, source_target_pairs={{0,1},{2,3},{4,5},{6,7},{8,9},{10,11},{12,13},{14,15},{16,17},{18,... | collective-permute-start | bytes 49160 | tf_op jit(solution)/shard_map/ppermute | solution.py:24
  50.2 3.1 %collective-permute-start.1 = (f32[128,32]{1,0:T(8,128)S(1)}, f32[128,32]{1,0:T(8,128)S(1)}, u32[]{:S(2)}, u32[]{:S(2)}) collective-permute-start(f32[128,32]{1,0:T(8,128)S(1)} %get-tuple-element.180), channel_id=1, source_target_pairs={{1,0},{3,2},{5,4},{7,6},{9,8},{11,10},{13,12},{15,14},{17,16},{19,... | collective-permute-start | bytes 49160 | tf_op jit(solution)/shard_map/ppermute | solution.py:27
  112.7 26.7 %all-to-all-start = ((bf16[1,256,4,512]{3,2,0,1:T(4,128)(2,1)}), bf16[1,256,4,512]{3,2,0,1:T(4,128)(2,1)}, u32[]{:S(2)}, u32[]{:S(2)}) async-start(bf16[1,256,4,512]{3,2,0,1:T(4,128)(2,1)} %copy.40), calls=%async_computation | async-start | bytes 2097152 | tf_op jit(solution)/shard_map/all_to_all | solution.py:136
  146.9 6.0 %copy-start = (bf16[1,2,64,8,2,2,128]{2,3,0,6,4,1,5:T(8,128)(2,1)}, bf16[1,2,64,8,2,2,128]{2,3,0,6,4,1,5:T(8,128)(2,1)S(1)}, u32[]{:S(2)}) copy-start(bf16[1,2,64,8,2,2,128]{2,3,0,6,4,1,5:T(8,128)(2,1)S(1)} %broadcast_multiply_fusion) | copy-start | bytes 3145732
  174.0 7.8 %copy-start.1 = (bf16[512,512]{1,0:T(8,128)(2,1)S(1)}, bf16[512,512]{1,0:T(8,128)(2,1)}, u32[]{:S(2)}) copy-start(bf16[512,512]{1,0:T(8,128)(2,1)} %get-tuple-element.181) | copy-start | bytes 1572868
  174.0 7.8 %copy-start.2 = (bf16[512,512]{1,0:T(8,128)(2,1)S(1)}, bf16[512,512]{1,0:T(8,128)(2,1)}, u32[]{:S(2)}) copy-start(bf16[512,512]{1,0:T(8,128)(2,1)} %get-tuple-element.182) | copy-start | bytes 1572868
Sparse Core Ops, SparseCore 0:
  55.6 54.0 all-reduce.1
where the time goes:
time: 197 us; the launch traced here: 196 us
  waiting for transfers between devices  55.3 us (28%)
  matrix products  47.8 us (24%)
  local copies, waits for them, and re-layouts  31.2 us (16%)
  other arithmetic  27.4 us (14%)
  between operations  13.6 us (7%)
  blocking collectives  12 us (6%)
  starting transfers between devices  7.95 us (4%)
    psum x1, waiting for transfers between devices, shards(): sources = lax.psum(local_terms.astype(jnp.bfloat16), 'rx')  53.5 us
    dot_general x15, matrix products, accumulate(): jnp.dot(trace_piece, base_table, preferred_element_type=jnp.float32)  18.9 us
    concatenate x2, local copies, waits for them, and re-layouts, shards(): jnp.concatenate([cross_real.reshape(src_local, chan_count, BAND), cross_i...  15.5 us
    all_gather x1, blocking collectives, shards(): lax.all_gather(whitened[None], ('tw', 'fq'), axis=0, tiled=True)  12 us
    another operation x2, other arithmetic  10.3 us
    dot_general x1, matrix products, shards(): jnp.einsum(pattern, src_imag, rec_real, preferred_element_type=jnp.float32)  9.08 us
    dot_general x1, matrix products, shards(): jnp.dot(stacked.reshape(src_local * chan_count, 2 * BAND), inv_table, pre...  7.22 us
    add x15, other arithmetic, accumulate(): return running + jnp.stack([new_real, new_imag], axis=2)  6.72 us
  transfers between devices with their start and end apart: 4, of which 2 were waited for; matrix products, arithmetic and copies ran while one was open for 6% of the time, Pallas kernels for 0%

commit v1 on v0

v1 whole, which is shorter than its diff:
```python
import math

import numpy as np
import jax
import jax.numpy as jnp
from jax import lax
from jax.experimental import pallas as pl
from jax.experimental.pallas import tpu as pltpu
from jax.sharding import PartitionSpec as P

NT = 15360
BAND = 512
F0 = 60
HW = 32
LAGS = 512
BLOCK = 1024
LANE = 128
KB = BAND // LANE
EPS = 1e-05


def tiled_columns(real, imag):
    rows = real.shape[0]
    pair = np.stack([real.reshape(rows, KB, LANE), imag.reshape(rows, KB, LANE)], axis=2)
    return pair.reshape(rows, 2 * BAND)


def forward_table():
    bins = F0 + np.arange(BAND)
    phase = np.arange(BLOCK)[:, None] * bins[None, :] % NT
    angle = phase * (2.0 * math.pi / NT)
    return tiled_columns(np.cos(angle), -np.sin(angle)).astype(jnp.bfloat16)


def turn_table():
    bins = F0 + np.arange(BAND)
    phase = BLOCK * np.arange(NT // BLOCK)[:, None] * bins[None, :] % NT
    angle = phase * (2.0 * math.pi / NT)
    return tiled_columns(np.cos(angle), -np.sin(angle)).astype(np.float32)


def inverse_table():
    bins = F0 + np.arange(BAND)
    phase = (np.arange(LAGS)[:, None] - LAGS // 2) * bins[None, :] % NT
    angle = phase * (2.0 * math.pi / NT)
    return np.ascontiguousarray(tiled_columns(np.cos(angle), -np.sin(angle)).T).astype(jnp.bfloat16)


def spectra_kernel(pos_ref, trace_ref, coef_ref, turn_ref, out_ref, spec_ref):
    step = pl.program_id(0)
    wins, chans, samples = trace_ref.shape
    rows = wins * chans
    blocks = samples // BLOCK
    pieces = [
        trace_ref[w, :, b * BLOCK : (b + 1) * BLOCK] for b in range(blocks) for w in range(wins)
    ]
    part = jnp.dot(
        jnp.concatenate(pieces, axis=0), coef_ref[...], preferred_element_type=jnp.float32
    )
    acc_re = part[:rows, :LANE]
    acc_im = part[:rows, LANE:]
    for b in range(1, blocks):
        re = part[b * rows : (b + 1) * rows, :LANE]
        im = part[b * rows : (b + 1) * rows, LANE:]
        turn_re = turn_ref[b : b + 1, :LANE]
        turn_im = turn_ref[b : b + 1, LANE:]
        acc_re = acc_re + (re * turn_re - im * turn_im)
        acc_im = acc_im + (re * turn_im + im * turn_re)
    spec_ref[step, 0] = acc_re
    spec_ref[step, 1] = acc_im

    @pl.when(step == KB - 1)
    def _():
        power = jnp.concatenate(
            [
                spec_ref[k, 0] * spec_ref[k, 0] + spec_ref[k, 1] * spec_ref[k, 1]
                for k in range(KB)
            ],
            axis=1,
        )
        high = power.astype(jnp.bfloat16)
        rest = power - high.astype(jnp.float32)
        middle = rest.astype(jnp.bfloat16)
        low = (rest - middle.astype(jnp.float32)).astype(jnp.bfloat16)
        row_ids = lax.broadcasted_iota(jnp.int32, (BAND, BAND), 0)
        col_ids = lax.broadcasted_iota(jnp.int32, (BAND, BAND), 1)
        box = jnp.where(jnp.abs(row_ids - col_ids) <= HW, 1.0, 0.0).astype(jnp.bfloat16)
        sums = jnp.dot(
            jnp.concatenate([high, middle, low], axis=0), box, preferred_element_type=jnp.float32
        )
        smooth = (sums[:rows] + (sums[rows : 2 * rows] + sums[2 * rows :])) / (2 * HW + 1)
        gain = lax.rsqrt(smooth + EPS)
        for k in range(KB):
            for p in range(2):
                white = spec_ref[k, p] * gain[:, k * LANE : (k + 1) * LANE]
                out_ref[:, :, (2 * k + p) * LANE : (2 * k + p + 1) * LANE] = white.astype(
                    jnp.bfloat16
                ).reshape(wins, chans, LANE)


def spectra(traces, fq_pos, fq_count):
    win_count, chans, samples = traces.shape
    wins = win_count // fq_count
    blocks = samples // BLOCK
    grid_spec = pltpu.PrefetchScalarGridSpec(
        num_scalar_prefetch=1,
        grid=(KB,),
        in_specs=[
            pl.BlockSpec((wins, chans, samples), lambda k, pos: (pos[0], 0, 0)),
            pl.BlockSpec((BLOCK, 2 * LANE), lambda k, pos: (0, k)),
            pl.BlockSpec((blocks, 2 * LANE), lambda k, pos: (0, k)),
        ],
        out_specs=pl.BlockSpec((wins, chans, 2 * BAND), lambda k, pos: (0, 0, 0)),
        scratch_shapes=[pltpu.VMEM((KB, 2, wins * chans, LANE), jnp.float32)],
    )
    return pl.pallas_call(
        spectra_kernel,
        grid_spec=grid_spec,
        out_shape=jax.ShapeDtypeStruct((wins, chans, 2 * BAND), jnp.bfloat16),
        name="spectra",
    )(fq_pos.reshape(1), traces, jnp.asarray(forward_table()), jnp.asarray(turn_table()))


def cross_kernel(sizes, *refs):
    groups, z_parts, wins, chans, src_local = sizes
    count = groups * z_parts
    block_refs = refs[:count]
    pick_ref, rate_ref, inv_ref, out_ref, src_ref, rec_ref, stack_ref = refs[count:]
    windows = groups * wins
    for g in range(groups):
        for w in range(wins):
            rows = jnp.concatenate(
                [
                    block_refs[g * z_parts + z][i * wins + w]
                    for z in range(z_parts)
                    for i in range(block_refs[g * z_parts + z].shape[0] // wins)
                ],
                axis=0,
            )
            chosen = jnp.dot(pick_ref[g * wins + w], rows, preferred_element_type=jnp.float32)
            for k in range(KB):
                re = chosen[:, 2 * k * LANE : (2 * k + 1) * LANE]
                im = chosen[:, (2 * k + 1) * LANE : (2 * k + 2) * LANE]
                s_re, s_im = re[:src_local], im[:src_local]
                r_re, r_im = re[src_local:], im[src_local:]
                src_ref[g * wins + w, k, 0] = s_re + s_im
                src_ref[g * wins + w, k, 1] = s_re
                src_ref[g * wins + w, k, 2] = s_im
                rec_ref[g * wins + w, k, 0] = r_re
                rec_ref[g * wins + w, k, 1] = r_im + r_re
                rec_ref[g * wins + w, k, 2] = r_im - r_re
    tiles = chans // 8

    def one_tile(index, carry):
        k = index // tiles
        tile = index % tiles
        rec = [
            [rec_ref[w, k, v, pl.ds(pl.multiple_of(tile * 8, 8), 8), :] for v in range(3)]
            for w in range(windows)
        ]

        def source_pair(pair, inner):
            both = []
            for half in range(2):
                s = pair * 2 + half
                sums = [None] * 3
                for w in range(windows):
                    for v in range(3):
                        row = src_ref[w, k, v, pl.ds(s, 8, stride=0), :]
                        term = row * rec[w][v]
                        sums[v] = term if w == 0 else sums[v] + term
                rate = rate_ref[s, pl.ds(pl.multiple_of(tile * 8, 8), 8), :]
                both.append(((sums[0] + sums[2]) * rate, (sums[1] - sums[0]) * rate))
            row = pl.multiple_of((pair * tiles + tile) * 16, 16)
            for p in range(2):
                stack_ref[2 * k + p, pl.ds(row, 16), :] = jnp.concatenate(
                    [both[0][p], both[1][p]], axis=0
                ).astype(jnp.bfloat16)
            return inner

        return lax.fori_loop(0, src_local // 2, source_pair, carry, unroll=2)

    lax.fori_loop(0, KB * tiles, one_tile, 0)
    scale = 1.0 / math.sqrt(BAND)
    chunk = min(8, src_local // 2)
    for first in range(0, src_local // 2, chunk):
        span = chunk * tiles * 16
        left = jnp.concatenate(
            [stack_ref[j, first * tiles * 16 : first * tiles * 16 + span, :] for j in range(2 * KB)],
            axis=1,
        )
        summed = jnp.dot(left, inv_ref[...], preferred_element_type=jnp.float32) * scale
        for i in range(chunk):
            for half in range(2):
                pieces = [
                    summed[((i * tiles + t) * 2 + half) * 8 : ((i * tiles + t) * 2 + half + 1) * 8]
                    for t in range(tiles)
                ]
                out_ref[2 * (first + i) + half] = jnp.concatenate(pieces, axis=0).astype(
                    jnp.bfloat16
                )


def shifted(value, axis, distance):
    count = lax.axis_size(axis)
    return lax.ppermute(value, axis, [(i, (i + distance) % count) for i in range(count)])


def shards(traces, src_index, valid):
    win_count, chans, _ = traces.shape
    rx_count, tw_count, fq_count = (lax.axis_size(a) for a in ("rx", "tw", "fq"))
    rx_pos, tw_pos, fq_pos = (lax.axis_index(a) for a in ("rx", "tw", "fq"))
    wins = win_count // fq_count
    own = spectra(traces, fq_pos, fq_count)

    along_z = [own] + [shifted(own, "rx", d) for d in range(1, rx_count)]
    if rx_count > 4:
        along_z = [jnp.concatenate(along_z, axis=0)]
    groups = [along_z]
    for d in range(1, tw_count):
        groups.append([shifted(v, "tw", d) for v in along_z])
    for d in range(1, fq_count):
        groups = groups + [[shifted(v, "fq", d) for v in g] for g in groups]
    z_parts = len(along_z)

    valid_float = valid.astype(jnp.float32)
    src_total = src_index.size
    src_local = src_total // (tw_count * fq_count)
    own_block = tw_pos * fq_count + fq_pos
    own_src = lax.dynamic_slice_in_dim(src_index.reshape(-1), own_block * src_local, src_local, 0)
    own_rec = rx_pos * chans + jnp.arange(chans, dtype=jnp.int32)
    wanted = jnp.concatenate([own_src, own_rec])
    channel_ids = (
        (rx_pos - jnp.arange(rx_count, dtype=jnp.int32)[:, None]) % rx_count * chans
        + jnp.arange(chans, dtype=jnp.int32)[None, :]
    ).reshape(-1)
    channel_total = rx_count * chans
    window_ids = []
    for f in range(fq_count):
        for t in range(tw_count):
            block = (tw_pos - t) % tw_count * fq_count + (fq_pos - f) % fq_count
            window_ids.append(block * wins + jnp.arange(wins, dtype=jnp.int32))
    window_ids = jnp.concatenate(window_ids)
    windows = window_ids.shape[0]
    use = (
        (window_ids[:, None] == jnp.arange(windows, dtype=jnp.int32)[None, :]).astype(jnp.float32)
        @ valid_float
    )
    spread = (wanted[:, None] == jnp.arange(channel_total, dtype=jnp.int32)[None, :]).astype(
        jnp.float32
    )
    use_wanted = jnp.dot(use, spread.T, preferred_element_type=jnp.float32)
    pick = jnp.where(
        wanted[None, :, None] == channel_ids[None, None, :], use_wanted[:, :, None], 0.0
    ).astype(jnp.bfloat16)
    pair_count = jnp.dot(
        use_wanted[:, :src_local].T, use_wanted[:, src_local:], preferred_element_type=jnp.float32
    )
    rate = jnp.broadcast_to(
        (1.0 / jnp.maximum(pair_count, 1.0))[:, :, None], (src_local, chans, LANE)
    )

    operands = [v for g in groups for v in g]
    sizes = (len(groups), z_parts, wins, chans, src_local)
    return pl.pallas_call(
        lambda *refs: cross_kernel(sizes, *refs),
        out_shape=jax.ShapeDtypeStruct((src_local, chans, LAGS), jnp.bfloat16),
        scratch_shapes=[
            pltpu.VMEM((windows, KB, 3, src_local, LANE), jnp.float32),
            pltpu.VMEM((windows, KB, 3, chans, LANE), jnp.float32),
            pltpu.VMEM((2 * KB, src_local * chans, LANE), jnp.bfloat16),
        ],
        name="cross",
    )(*operands, pick, rate, jnp.asarray(inverse_table()))


def solution(mesh):
    return jax.shard_map(
        shards,
        mesh=mesh,
        in_specs=(P("tw", ("grp", "rx"), None), P("grp", None), P(None, "grp")),
        out_specs=P(("tw", "fq"), ("grp", "rx"), None),
        check_vma=False,
    )
```

time: 197 us -> 52.3 us (0.27)
  matrix products: 47.8 us -> 0.55 us
  waiting for transfers between devices: 55.3 us -> 14.5 us
  local copies, waits for them, and re-layouts: 31.2 us -> 1.71 us
  other arithmetic: 27.4 us -> 1.17 us
  Pallas kernels: 0 us -> 22.9 us
  between operations: 13.6 us -> 0.22 us
  blocking collectives: 12 us -> 0 us
  starting transfers between devices: 7.95 us -> 11 us
    psum x1 -> x0, waiting for transfers between devices: 53.5 us -> none  [shards(): sources = lax.psum(local_terms.astype(jnp.bfloat16), 'rx')]
    dot_general x24 -> x2, matrix products: 47.8 us -> 0.55 us  [the longest x1 0.29 us: shards(): use_wanted = jnp.dot(use, spread.T, preferred_element_type=jnp.float32)]
    pallas_call x0 -> x2, Pallas kernels: none -> 22.9 us  [the longest x1 17.1 us: shards(): pl.pallas_call(lambda *refs: cross_kernel(sizes, *refs), out_shape=jax.Sh...]
    concatenate x2 -> x0, local copies, waits for them, and re-layouts: 15.5 us -> none  [shards(): jnp.concatenate([cross_real.reshape(src_local, chan_count, BAND), cross_i...]
    ppermute x2 -> x15, waiting for transfers between devices: 1.74 us -> 14.5 us  [shifted(): lax.ppermute(value, axis, [(i, (i + distance) % count) for i in range(cou...]
    all_gather x1 -> x0, blocking collectives: 12 us -> none  [shards(): lax.all_gather(whitened[None], ('tw', 'fq'), axis=0, tiled=True)]
    reshape x19 -> x1, local copies, waits for them, and re-layouts: 10.9 us -> 0.08 us  [shards(): src_index.reshape(-1)]
    another operation x3 -> x0, other arithmetic: 10.4 us -> none
  transfers between devices with their start and end apart: 4 -> 15, of which waited for: 2 -> 5; matrix products, arithmetic and copies ran while one was open for 6% -> 4% of each run, Pallas kernels for 0% -> 0%
where the time goes in v1:
time: 52.3 us; the launch traced here: 52.1 us
  Pallas kernels  22.9 us (44%)
  waiting for transfers between devices  14.5 us (28%)
  starting transfers between devices  11 us (21%)
  local copies, waits for them, and re-layouts  1.71 us (3%)
  other arithmetic  1.17 us (2%)
  matrix products  0.55 us (1%)
    pallas_call x1, Pallas kernels, shards(): pl.pallas_call(lambda *refs: cross_kernel(sizes, *refs), out_shape=jax.Sh...  17.1 us
    ppermute x15, waiting for transfers between devices, shifted(): lax.ppermute(value, axis, [(i, (i + distance) % count) for i in range(cou...  14.5 us
    ppermute x15, starting transfers between devices, shifted(): lax.ppermute(value, axis, [(i, (i + distance) % count) for i in range(cou...  11 us
    pallas_call x1, Pallas kernels, spectra(): pl.pallas_call(spectra_kernel, grid_spec=grid_spec, out_shape=jax.ShapeDt...  5.86 us
    broadcast_in_dim x1, local copies, waits for them, and re-layouts, shards(): jnp.broadcast_to((1.0 / jnp.maximum(pair_count, 1.0))[:, :, None], (src_l...  1.31 us
  transfers between devices with their start and end apart: 15, of which 5 were waited for; matrix products, arithmetic and copies ran while one was open for 4% of the time, Pallas kernels for 0%

profile of v1, /device:TPU:0, one launch (start us, length us, event | category | flops | bytes accessed | tf_op | source)
XLA Modules:
  0.0 52.1 jit_solution(4793682464493710436)
XLA Ops:
  0.0 5.9 %spectra.1.refs_0_ = bf16[2,32,1024]{2,1,0:T(8,128)(2,1)} custom-call(s32[1]{0:T(128)} %bitcast.pos_ref, bf16[4,32,15360]{2,1,0:T(8,128)(2,1)} %trace_ref.1, bf16[1024,1024]{1,0:T(8,128)(2,1)} %constant.80.clone.coef_ref, f32[15,1024]{1,0:T(8,128)} %constant.81.clone.turn_ref), custom_call_target="tpu_custom_call" | custom-call | tf_op jit(solution)/shard_map/spectra/pallas_call | solution.py:116
  5.9 0.5 collective-permute-start.7
  6.4 2.5 %collective-permute-start.3 = (bf16[2,32,1024]{2,1,0:T(8,128)(2,1)}, bf16[2,32,1024]{2,1,0:T(8,128)(2,1)S(1)}, u32[]{:S(2)}, u32[]{:S(2)}) collective-permute-start(bf16[2,32,1024]{2,1,0:T(8,128)(2,1)} %spectra.1.refs_0_), channel_id=1, source_target_pairs={{0,2},{2,0},{1,3},{3,1},{4,6},{6,4},{5,7},{7,5},{8,10},{10,8},{9,1... | collective-permute-start | bytes 393224 | tf_op jit(solution)/shard_map/ppermute | solution.py:206
  8.8 3.6 %collective-permute-start.2 = (bf16[2,32,1024]{2,1,0:T(8,128)(2,1)}, bf16[2,32,1024]{2,1,0:T(8,128)(2,1)S(1)}, u32[]{:S(2)}, u32[]{:S(2)}) collective-permute-start(bf16[2,32,1024]{2,1,0:T(8,128)(2,1)} %spectra.1.refs_0_), channel_id=1, source_target_pairs={{0,12},{4,0},{8,4},{12,8},{1,13},{5,1},{9,5},{13,9},{2,14},{6,2},{... | collective-permute-start | bytes 393224 | tf_op jit(solution)/shard_map/ppermute | solution.py:206
  12.4 0.0 collective-permute-start.1
  12.4 1.0 %collective-permute-start = (bf16[2,32,1024]{2,1,0:T(8,128)(2,1)}, bf16[2,32,1024]{2,1,0:T(8,128)(2,1)S(1)}, u32[]{:S(2)}, u32[]{:S(2)}) collective-permute-start(bf16[2,32,1024]{2,1,0:T(8,128)(2,1)} %spectra.1.refs_0_), channel_id=1, source_target_pairs={{0,4},{4,8},{8,12},{12,0},{1,5},{5,9},{9,13},{13,1},{2,6},{6,10},{... | collective-permute-start | bytes 393224 | tf_op jit(solution)/shard_map/ppermute | solution.py:206
  13.5 0.0 copy-done.15
  13.5 0.1 reshape.80
  13.6 0.1 iota_add_fusion
  13.6 0.1 add.106
  13.7 0.1 dynamic_slice.3
  13.8 0.1 pad_add_fusion
  13.9 0.1 pad_add_fusion.1
  14.0 0.3 fusion.1
  14.2 0.3 fusion
  14.5 0.1 copy.7
  14.6 2.1 %collective-permute-done.2.refs_3_ = bf16[2,32,1024]{2,1,0:T(8,128)(2,1)S(1)} collective-permute-done((bf16[2,32,1024]{2,1,0:T(8,128)(2,1)}, bf16[2,32,1024]{2,1,0:T(8,128)(2,1)S(1)}, u32[]{:S(2)}, u32[]{:S(2)}) %collective-permute-start.2) | collective-permute-done | bytes 131104 | tf_op jit(solution)/shard_map/ppermute | solution.py:206
  16.7 0.0 collective-permute-start.10
  16.7 0.0 collective-permute-done.7.refs_8_
  16.7 0.6 %collective-permute-start.6 = (bf16[2,32,1024]{2,1,0:T(8,128)(2,1)S(1)}, bf16[2,32,1024]{2,1,0:T(8,128)(2,1)S(1)}, u32[]{:S(2)}, u32[]{:S(2)}) collective-permute-start(bf16[2,32,1024]{2,1,0:T(8,128)(2,1)S(1)} %collective-permute-done.2.refs_3_), channel_id=1, source_target_pairs={{0,2},{2,0},{1,3},{3,1},{4,6},{6,4},{5,7},{7,5},{8,10},{10,8},{9,1... | collective-permute-start | bytes 393224 | tf_op jit(solution)/shard_map/ppermute | solution.py:206
  17.3 0.0 collective-permute-done.3.refs_4_
  17.3 0.2 collective-permute-start.11
  17.5 6.9 %collective-permute-done.1.refs_2_ = bf16[2,32,1024]{2,1,0:T(8,128)(2,1)S(1)} collective-permute-done((bf16[2,32,1024]{2,1,0:T(8,128)(2,1)}, bf16[2,32,1024]{2,1,0:T(8,128)(2,1)S(1)}, u32[]{:S(2)}, u32[]{:S(2)}) %collective-permute-start.1) | collective-permute-done | bytes 131104 | tf_op jit(solution)/shard_map/ppermute | solution.py:206
  24.4 0.5 %collective-permute-start.5 = (bf16[2,32,1024]{2,1,0:T(8,128)(2,1)S(1)}, bf16[2,32,1024]{2,1,0:T(8,128)(2,1)S(1)}, u32[]{:S(2)}, u32[]{:S(2)}) collective-permute-start(bf16[2,32,1024]{2,1,0:T(8,128)(2,1)S(1)} %collective-permute-done.1.refs_2_), channel_id=1, source_target_pairs={{0,2},{2,0},{1,3},{3,1},{4,6},{6,4},{5,7},{7,5},{8,10},{10,8},{9,1... | collective-permute-start | bytes 393224 | tf_op jit(solution)/shard_map/ppermute | solution.py:206
  25.0 0.0 collective-permute-done.refs_1_
  25.0 1.5 %collective-permute-start.4 = (bf16[2,32,1024]{2,1,0:T(8,128)(2,1)S(1)}, bf16[2,32,1024]{2,1,0:T(8,128)(2,1)S(1)}, u32[]{:S(2)}, u32[]{:S(2)}) collective-permute-start(bf16[2,32,1024]{2,1,0:T(8,128)(2,1)S(1)} %collective-permute-done.refs_1_), channel_id=1, source_target_pairs={{0,2},{2,0},{1,3},{3,1},{4,6},{6,4},{5,7},{7,5},{8,10},{10,8},{9,1... | collective-permute-start | bytes 393224 | tf_op jit(solution)/shard_map/ppermute | solution.py:206
  26.5 0.1 broadcast_compare_fusion
  26.6 0.0 collective-permute-done.11.refs_12_
  26.6 0.0 copy-start.7
  26.6 0.1 collective-permute-start.9
  26.7 0.0 collective-permute-done.10.refs_11_
  26.7 0.5 collective-permute-start.8
  27.2 0.0 collective-permute-done.6.refs_7_
  27.2 0.1 collective-permute-start.14
  27.3 3.5 %collective-permute-done.5.refs_6_ = bf16[2,32,1024]{2,1,0:T(8,128)(2,1)S(1)} collective-permute-done((bf16[2,32,1024]{2,1,0:T(8,128)(2,1)S(1)}, bf16[2,32,1024]{2,1,0:T(8,128)(2,1)S(1)}, u32[]{:S(2)}, u32[]{:S(2)}) %collective-permute-start.5) | collective-permute-done | bytes 131104 | tf_op jit(solution)/shard_map/ppermute | solution.py:206
  30.8 0.0 collective-permute-start.13
  30.8 1.4 %collective-permute-done.4.refs_5_ = bf16[2,32,1024]{2,1,0:T(8,128)(2,1)S(1)} collective-permute-done((bf16[2,32,1024]{2,1,0:T(8,128)(2,1)S(1)}, bf16[2,32,1024]{2,1,0:T(8,128)(2,1)S(1)}, u32[]{:S(2)}, u32[]{:S(2)}) %collective-permute-start.4) | collective-permute-done | bytes 131104 | tf_op jit(solution)/shard_map/ppermute | solution.py:206
  32.3 0.0 collective-permute-start.12
  32.3 0.8 %select_convert_fusion.refs_16_ = bf16[8,96,128]{2,1,0:T(8,128)(2,1)} fusion(bf16[8,96]{1,0:T(8,128)(2,1)S(1)} %fusion.1, pred[96,128]{1,0:T(8,128)(4,1)S(1)} %broadcast_compare_fusion), kind=kLoop, calls=%fused_computation.4 | loop fusion | flops 98304 | bytes 210432 | tf_op jit(solution)/shard_map/convert_element_type | solution.py:255
  33.1 0.0 collective-permute-done.9.refs_10_
  33.1 0.0 collective-permute-done.8.refs_9_
  33.1 0.0 copy-start.11
  33.1 0.0 collective-permute-done.14.refs_15_
  33.2 0.0 collective-permute-done.13.refs_14_
  33.2 0.4 collective-permute-done.12.refs_13_
  33.6 1.3 %broadcast_in_dim.25.refs_17_ = f32[64,32,128]{2,1,0:T(8,128)} broadcast(f32[64,32]{1,0:T(8,128)S(1)} %copy.7), dimensions={0,1} | broadcast | bytes 1056768 | tf_op jit(solution)/shard_map/broadcast_in_dim | solution.py:259
  34.9 0.0 copy-done
  35.0 17.1 %cross.1 = bf16[64,32,512]{2,1,0:T(8,128)(2,1)} custom-call(bf16[2,32,1024]{2,1,0:T(8,128)(2,1)} %spectra.1.refs_0_, bf16[2,32,1024]{2,1,0:T(8,128)(2,1)} %copy-done.4, bf16[2,32,1024]{2,1,0:T(8,128)(2,1)} %copy-done.3, bf16[2,32,1024]{2,1,0:T(8,128)(2,1)} %copy-done.2, bf16[2,32,1024]{2,1,0:T(8,128)(2,1)} %copy-done.1, bf16[2,32,1024]{2,1,0:T(8,128)(2,1)} %copy-done.9, ...), custom_call_target="tpu_custom_call" | custom-call | tf_op jit(solution)/shard_map/cross/pallas_call | solution.py:265
  (34 shorter events, 0.1 us)
Async XLA Ops:
  0.0 13.5 %copy-start.15 = (s32[4,64]{1,0:T(4,128)S(1)}, s32[4,64]{1,0:T(4,128)}, u32[]{:S(2)}) copy-start(s32[4,64]{1,0:T(4,128)} %param.7) | copy-start | bytes 3076
  0.0 14.0 %copy-start.16 = (s32[8,128]{1,0:T(8,128)S(1)}, s32[8,128]{1,0:T(8,128)}, u32[]{:S(2)}) copy-start(s32[8,128]{1,0:T(8,128)} %param.8) | copy-start | bytes 12292
  5.9 10.9 %collective-permute-start.7 = (bf16[2,32,1024]{2,1,0:T(8,128)(2,1)}, bf16[2,32,1024]{2,1,0:T(8,128)(2,1)S(1)}, u32[]{:S(2)}, u32[]{:S(2)}) collective-permute-start(bf16[2,32,1024]{2,1,0:T(8,128)(2,1)} %spectra.1.refs_0_), channel_id=1, source_target_pairs={{0,1},{1,0},{2,3},{3,2},{4,5},{5,4},{6,7},{7,6},{8,9},{9,8},{10,11... | collective-permute-start | bytes 393224 | tf_op jit(solution)/shard_map/ppermute | solution.py:206
  6.4 11.0 %collective-permute-start.3 = (bf16[2,32,1024]{2,1,0:T(8,128)(2,1)}, bf16[2,32,1024]{2,1,0:T(8,128)(2,1)S(1)}, u32[]{:S(2)}, u32[]{:S(2)}) collective-permute-start(bf16[2,32,1024]{2,1,0:T(8,128)(2,1)} %spectra.1.refs_0_), channel_id=1, source_target_pairs={{0,2},{2,0},{1,3},{3,1},{4,6},{6,4},{5,7},{7,5},{8,10},{10,8},{9,1... | collective-permute-start | bytes 393224 | tf_op jit(solution)/shard_map/ppermute | solution.py:206
  8.8 7.9 %collective-permute-start.2 = (bf16[2,32,1024]{2,1,0:T(8,128)(2,1)}, bf16[2,32,1024]{2,1,0:T(8,128)(2,1)S(1)}, u32[]{:S(2)}, u32[]{:S(2)}) collective-permute-start(bf16[2,32,1024]{2,1,0:T(8,128)(2,1)} %spectra.1.refs_0_), channel_id=1, source_target_pairs={{0,12},{4,0},{8,4},{12,8},{1,13},{5,1},{9,5},{13,9},{2,14},{6,2},{... | collective-permute-start | bytes 393224 | tf_op jit(solution)/shard_map/ppermute | solution.py:206
  12.4 12.0 %collective-permute-start.1 = (bf16[2,32,1024]{2,1,0:T(8,128)(2,1)}, bf16[2,32,1024]{2,1,0:T(8,128)(2,1)S(1)}, u32[]{:S(2)}, u32[]{:S(2)}) collective-permute-start(bf16[2,32,1024]{2,1,0:T(8,128)(2,1)} %spectra.1.refs_0_), channel_id=1, source_target_pairs={{0,8},{4,12},{8,0},{12,4},{1,9},{5,13},{9,1},{13,5},{2,10},{6,14},... | collective-permute-start | bytes 393224 | tf_op jit(solution)/shard_map/ppermute | solution.py:206
  12.4 12.5 %collective-permute-start = (bf16[2,32,1024]{2,1,0:T(8,128)(2,1)}, bf16[2,32,1024]{2,1,0:T(8,128)(2,1)S(1)}, u32[]{:S(2)}, u32[]{:S(2)}) collective-permute-start(bf16[2,32,1024]{2,1,0:T(8,128)(2,1)} %spectra.1.refs_0_), channel_id=1, source_target_pairs={{0,4},{4,8},{8,12},{12,0},{1,5},{5,9},{9,13},{13,1},{2,6},{6,10},{... | collective-permute-start | bytes 393224 | tf_op jit(solution)/shard_map/ppermute | solution.py:206
  16.7 18.2 %copy-start.2 = (bf16[2,32,1024]{2,1,0:T(8,128)(2,1)}, bf16[2,32,1024]{2,1,0:T(8,128)(2,1)S(1)}, u32[]{:S(2)}) copy-start(bf16[2,32,1024]{2,1,0:T(8,128)(2,1)S(1)} %collective-permute-done.2.refs_3_) | copy-start | bytes 393220
  16.7 9.9 %collective-permute-start.10 = (bf16[2,32,1024]{2,1,0:T(8,128)(2,1)S(1)}, bf16[2,32,1024]{2,1,0:T(8,128)(2,1)S(1)}, u32[]{:S(2)}, u32[]{:S(2)}) collective-permute-start(bf16[2,32,1024]{2,1,0:T(8,128)(2,1)S(1)} %collective-permute-done.2.refs_3_), channel_id=1, source_target_pairs={{0,1},{1,0},{2,3},{3,2},{4,5},{5,4},{6,7},{7,6},{8,9},{9,8},{10,11... | collective-permute-start | bytes 393224 | tf_op jit(solution)/shard_map/ppermute | solution.py:206
  16.7 18.2 %copy-start = (bf16[2,32,1024]{2,1,0:T(8,128)(2,1)}, bf16[2,32,1024]{2,1,0:T(8,128)(2,1)S(1)}, u32[]{:S(2)}) copy-start(bf16[2,32,1024]{2,1,0:T(8,128)(2,1)S(1)} %collective-permute-done.7.refs_8_) | copy-start | bytes 393220
  16.7 10.4 %collective-permute-start.6 = (bf16[2,32,1024]{2,1,0:T(8,128)(2,1)S(1)}, bf16[2,32,1024]{2,1,0:T(8,128)(2,1)S(1)}, u32[]{:S(2)}, u32[]{:S(2)}) collective-permute-start(bf16[2,32,1024]{2,1,0:T(8,128)(2,1)S(1)} %collective-permute-done.2.refs_3_), channel_id=1, source_target_pairs={{0,2},{2,0},{1,3},{3,1},{4,6},{6,4},{5,7},{7,5},{8,10},{10,8},{9,1... | collective-permute-start | bytes 393224 | tf_op jit(solution)/shard_map/ppermute | solution.py:206
  17.3 17.6 %copy-start.1 = (bf16[2,32,1024]{2,1,0:T(8,128)(2,1)}, bf16[2,32,1024]{2,1,0:T(8,128)(2,1)S(1)}, u32[]{:S(2)}) copy-start(bf16[2,32,1024]{2,1,0:T(8,128)(2,1)S(1)} %collective-permute-done.3.refs_4_) | copy-start | bytes 393220
  17.3 9.2 %collective-permute-start.11 = (bf16[2,32,1024]{2,1,0:T(8,128)(2,1)S(1)}, bf16[2,32,1024]{2,1,0:T(8,128)(2,1)S(1)}, u32[]{:S(2)}, u32[]{:S(2)}) collective-permute-start(bf16[2,32,1024]{2,1,0:T(8,128)(2,1)S(1)} %collective-permute-done.3.refs_4_), channel_id=1, source_target_pairs={{0,1},{1,0},{2,3},{3,2},{4,5},{5,4},{6,7},{7,6},{8,9},{9,8},{10,11... | collective-permute-start | bytes 393224 | tf_op jit(solution)/shard_map/ppermute | solution.py:206
  24.4 10.5 %copy-start.3 = (bf16[2,32,1024]{2,1,0:T(8,128)(2,1)}, bf16[2,32,1024]{2,1,0:T(8,128)(2,1)S(1)}, u32[]{:S(2)}) copy-start(bf16[2,32,1024]{2,1,0:T(8,128)(2,1)S(1)} %collective-permute-done.1.refs_2_) | copy-start | bytes 393220
  24.4 6.4 %collective-permute-start.5 = (bf16[2,32,1024]{2,1,0:T(8,128)(2,1)S(1)}, bf16[2,32,1024]{2,1,0:T(8,128)(2,1)S(1)}, u32[]{:S(2)}, u32[]{:S(2)}) collective-permute-start(bf16[2,32,1024]{2,1,0:T(8,128)(2,1)S(1)} %collective-permute-done.1.refs_2_), channel_id=1, source_target_pairs={{0,2},{2,0},{1,3},{3,1},{4,6},{6,4},{5,7},{7,5},{8,10},{10,8},{9,1... | collective-permute-start | bytes 393224 | tf_op jit(solution)/shard_map/ppermute | solution.py:206
  25.0 9.9 %copy-start.4 = (bf16[2,32,1024]{2,1,0:T(8,128)(2,1)}, bf16[2,32,1024]{2,1,0:T(8,128)(2,1)S(1)}, u32[]{:S(2)}) copy-start(bf16[2,32,1024]{2,1,0:T(8,128)(2,1)S(1)} %collective-permute-done.refs_1_) | copy-start | bytes 393220
  25.0 7.3 %collective-permute-start.4 = (bf16[2,32,1024]{2,1,0:T(8,128)(2,1)S(1)}, bf16[2,32,1024]{2,1,0:T(8,128)(2,1)S(1)}, u32[]{:S(2)}, u32[]{:S(2)}) collective-permute-start(bf16[2,32,1024]{2,1,0:T(8,128)(2,1)S(1)} %collective-permute-done.refs_1_), channel_id=1, source_target_pairs={{0,2},{2,0},{1,3},{3,1},{4,6},{6,4},{5,7},{7,5},{8,10},{10,8},{9,1... | collective-permute-start | bytes 393224 | tf_op jit(solution)/shard_map/ppermute | solution.py:206
  26.6 8.4 %copy-start.7 = (bf16[2,32,1024]{2,1,0:T(8,128)(2,1)}, bf16[2,32,1024]{2,1,0:T(8,128)(2,1)S(1)}, u32[]{:S(2)}) copy-start(bf16[2,32,1024]{2,1,0:T(8,128)(2,1)S(1)} %collective-permute-done.11.refs_12_) | copy-start | bytes 393220
  26.6 6.5 %collective-permute-start.9 = (bf16[2,32,1024]{2,1,0:T(8,128)(2,1)S(1)}, bf16[2,32,1024]{2,1,0:T(8,128)(2,1)S(1)}, u32[]{:S(2)}, u32[]{:S(2)}) collective-permute-start(bf16[2,32,1024]{2,1,0:T(8,128)(2,1)S(1)} %collective-permute-done.1.refs_2_), channel_id=1, source_target_pairs={{0,1},{1,0},{2,3},{3,2},{4,5},{5,4},{6,7},{7,6},{8,9},{9,8},{10,11... | collective-permute-start | bytes 393224 | tf_op jit(solution)/shard_map/ppermute | solution.py:206
  26.7 8.3 %copy-start.5 = (bf16[2,32,1024]{2,1,0:T(8,128)(2,1)}, bf16[2,32,1024]{2,1,0:T(8,128)(2,1)S(1)}, u32[]{:S(2)}) copy-start(bf16[2,32,1024]{2,1,0:T(8,128)(2,1)S(1)} %collective-permute-done.10.refs_11_) | copy-start | bytes 393220
  26.7 6.4 %collective-permute-start.8 = (bf16[2,32,1024]{2,1,0:T(8,128)(2,1)S(1)}, bf16[2,32,1024]{2,1,0:T(8,128)(2,1)S(1)}, u32[]{:S(2)}, u32[]{:S(2)}) collective-permute-start(bf16[2,32,1024]{2,1,0:T(8,128)(2,1)S(1)} %collective-permute-done.refs_1_), channel_id=1, source_target_pairs={{0,1},{1,0},{2,3},{3,2},{4,5},{5,4},{6,7},{7,6},{8,9},{9,8},{10,11... | collective-permute-start | bytes 393224 | tf_op jit(solution)/shard_map/ppermute | solution.py:206
  27.2 7.8 %copy-start.6 = (bf16[2,32,1024]{2,1,0:T(8,128)(2,1)}, bf16[2,32,1024]{2,1,0:T(8,128)(2,1)S(1)}, u32[]{:S(2)}) copy-start(bf16[2,32,1024]{2,1,0:T(8,128)(2,1)S(1)} %collective-permute-done.6.refs_7_) | copy-start | bytes 393220
  27.2 6.0 %collective-permute-start.14 = (bf16[2,32,1024]{2,1,0:T(8,128)(2,1)S(1)}, bf16[2,32,1024]{2,1,0:T(8,128)(2,1)S(1)}, u32[]{:S(2)}, u32[]{:S(2)}) collective-permute-start(bf16[2,32,1024]{2,1,0:T(8,128)(2,1)S(1)} %collective-permute-done.6.refs_7_), channel_id=1, source_target_pairs={{0,1},{1,0},{2,3},{3,2},{4,5},{5,4},{6,7},{7,6},{8,9},{9,8},{10,11... | collective-permute-start | bytes 393224 | tf_op jit(solution)/shard_map/ppermute | solution.py:206
  30.8 4.2 %copy-start.8 = (bf16[2,32,1024]{2,1,0:T(8,128)(2,1)}, bf16[2,32,1024]{2,1,0:T(8,128)(2,1)S(1)}, u32[]{:S(2)}) copy-start(bf16[2,32,1024]{2,1,0:T(8,128)(2,1)S(1)} %collective-permute-done.5.refs_6_) | copy-start | bytes 393220
  30.8 2.3 %collective-permute-start.13 = (bf16[2,32,1024]{2,1,0:T(8,128)(2,1)S(1)}, bf16[2,32,1024]{2,1,0:T(8,128)(2,1)S(1)}, u32[]{:S(2)}, u32[]{:S(2)}) collective-permute-start(bf16[2,32,1024]{2,1,0:T(8,128)(2,1)S(1)} %collective-permute-done.5.refs_6_), channel_id=1, source_target_pairs={{0,1},{1,0},{2,3},{3,2},{4,5},{5,4},{6,7},{7,6},{8,9},{9,8},{10,11... | collective-permute-start | bytes 393224 | tf_op jit(solution)/shard_map/ppermute | solution.py:206
  32.3 2.7 %copy-start.9 = (bf16[2,32,1024]{2,1,0:T(8,128)(2,1)}, bf16[2,32,1024]{2,1,0:T(8,128)(2,1)S(1)}, u32[]{:S(2)}) copy-start(bf16[2,32,1024]{2,1,0:T(8,128)(2,1)S(1)} %collective-permute-done.4.refs_5_) | copy-start | bytes 393220
  32.3 1.3 %collective-permute-start.12 = (bf16[2,32,1024]{2,1,0:T(8,128)(2,1)S(1)}, bf16[2,32,1024]{2,1,0:T(8,128)(2,1)S(1)}, u32[]{:S(2)}, u32[]{:S(2)}) collective-permute-start(bf16[2,32,1024]{2,1,0:T(8,128)(2,1)S(1)} %collective-permute-done.4.refs_5_), channel_id=1, source_target_pairs={{0,1},{1,0},{2,3},{3,2},{4,5},{5,4},{6,7},{7,6},{8,9},{9,8},{10,11... | collective-permute-start | bytes 393224 | tf_op jit(solution)/shard_map/ppermute | solution.py:206
  33.1 1.9 %copy-start.10 = (bf16[2,32,1024]{2,1,0:T(8,128)(2,1)}, bf16[2,32,1024]{2,1,0:T(8,128)(2,1)S(1)}, u32[]{:S(2)}) copy-start(bf16[2,32,1024]{2,1,0:T(8,128)(2,1)S(1)} %collective-permute-done.9.refs_10_) | copy-start | bytes 393220
  33.1 1.9 %copy-start.11 = (bf16[2,32,1024]{2,1,0:T(8,128)(2,1)}, bf16[2,32,1024]{2,1,0:T(8,128)(2,1)S(1)}, u32[]{:S(2)}) copy-start(bf16[2,32,1024]{2,1,0:T(8,128)(2,1)S(1)} %collective-permute-done.8.refs_9_) | copy-start | bytes 393220
  33.1 1.9 %copy-start.12 = (bf16[2,32,1024]{2,1,0:T(8,128)(2,1)}, bf16[2,32,1024]{2,1,0:T(8,128)(2,1)S(1)}, u32[]{:S(2)}) copy-start(bf16[2,32,1024]{2,1,0:T(8,128)(2,1)S(1)} %collective-permute-done.14.refs_15_) | copy-start | bytes 393220
  33.2 1.9 %copy-start.13 = (bf16[2,32,1024]{2,1,0:T(8,128)(2,1)}, bf16[2,32,1024]{2,1,0:T(8,128)(2,1)S(1)}, u32[]{:S(2)}) copy-start(bf16[2,32,1024]{2,1,0:T(8,128)(2,1)S(1)} %collective-permute-done.13.refs_14_) | copy-start | bytes 393220
  33.6 1.4 %copy-start.14 = (bf16[2,32,1024]{2,1,0:T(8,128)(2,1)}, bf16[2,32,1024]{2,1,0:T(8,128)(2,1)S(1)}, u32[]{:S(2)}) copy-start(bf16[2,32,1024]{2,1,0:T(8,128)(2,1)S(1)} %collective-permute-done.12.refs_13_) | copy-start | bytes 393220

commit v2 on v1

--- a/solution.py
+++ b/solution.py
@@ -16,6 +16,8 @@
 BLOCK = 1024
 LANE = 128
 KB = BAND // LANE
+SPLIT = 2
+LIMIT = 40 * 2**20
 EPS = 1e-05
 
 
@@ -121,106 +123,192 @@
     )(fq_pos.reshape(1), traces, jnp.asarray(forward_table()), jnp.asarray(turn_table()))
 
 
-def cross_kernel(sizes, *refs):
-    groups, z_parts, wins, chans, src_local = sizes
-    count = groups * z_parts
-    block_refs = refs[:count]
-    pick_ref, rate_ref, inv_ref, out_ref, src_ref, rec_ref, stack_ref = refs[count:]
-    windows = groups * wins
+def choose_rows(block_refs, pick_ref, src_ref, rec_ref, sizes, k):
+    groups, z_parts, wins, _, src_local = sizes
+    lanes = slice(k * 2 * LANE, (k + 1) * 2 * LANE)
     for g in range(groups):
         for w in range(wins):
             rows = jnp.concatenate(
                 [
-                    block_refs[g * z_parts + z][i * wins + w]
+                    block_refs[g * z_parts + z][i * wins + w, :, lanes]
                     for z in range(z_parts)
                     for i in range(block_refs[g * z_parts + z].shape[0] // wins)
                 ],
                 axis=0,
             )
             chosen = jnp.dot(pick_ref[g * wins + w], rows, preferred_element_type=jnp.float32)
-            for k in range(KB):
-                re = chosen[:, 2 * k * LANE : (2 * k + 1) * LANE]
-                im = chosen[:, (2 * k + 1) * LANE : (2 * k + 2) * LANE]
-                s_re, s_im = re[:src_local], im[:src_local]
-                r_re, r_im = re[src_local:], im[src_local:]
-                src_ref[g * wins + w, k, 0] = s_re + s_im
-                src_ref[g * wins + w, k, 1] = s_re
-                src_ref[g * wins + w, k, 2] = s_im
-                rec_ref[g * wins + w, k, 0] = r_re
-                rec_ref[g * wins + w, k, 1] = r_im + r_re
-                rec_ref[g * wins + w, k, 2] = r_im - r_re
-    tiles = chans // 8
-
-    def one_tile(index, carry):
-        k = index // tiles
-        tile = index % tiles
-        rec = [
-            [rec_ref[w, k, v, pl.ds(pl.multiple_of(tile * 8, 8), 8), :] for v in range(3)]
-            for w in range(windows)
-        ]
-
-        def source_pair(pair, inner):
-            both = []
-            for half in range(2):
-                s = pair * 2 + half
-                sums = [None] * 3
-                for w in range(windows):
-                    for v in range(3):
-                        row = src_ref[w, k, v, pl.ds(s, 8, stride=0), :]
-                        term = row * rec[w][v]
-                        sums[v] = term if w == 0 else sums[v] + term
-                rate = rate_ref[s, pl.ds(pl.multiple_of(tile * 8, 8), 8), :]
-                both.append(((sums[0] + sums[2]) * rate, (sums[1] - sums[0]) * rate))
-            row = pl.multiple_of((pair * tiles + tile) * 16, 16)
-            for p in range(2):
-                stack_ref[2 * k + p, pl.ds(row, 16), :] = jnp.concatenate(
-                    [both[0][p], both[1][p]], axis=0
-                ).astype(jnp.bfloat16)
-            return inner
-
-        return lax.fori_loop(0, src_local // 2, source_pair, carry, unroll=2)
-
-    lax.fori_loop(0, KB * tiles, one_tile, 0)
+            re, im = chosen[:, :LANE], chosen[:, LANE:]
+            s_re, s_im = re[:src_local], im[:src_local]
+            r_re, r_im = re[src_local:], im[src_local:]
+            src_ref[g * wins + w, 0] = s_re + s_im
+            src_ref[g * wins + w, 1] = s_re
+            src_ref[g * wins + w, 2] = s_im
+            rec_ref[g * wins + w, 0] = r_re
+            rec_ref[g * wins + w, 1] = r_im + r_re
+            rec_ref[g * wins + w, 2] = r_im - r_re
+
+
+def cross_sums(src_ref, s, recs):
+    sums = [[None] * 3 for _ in recs]
+    for w in range(len(recs[0])):
+        for v in range(3):
+            row = src_ref[w, v, pl.ds(s, 8, stride=0), :]
+            for total, rec in zip(sums, recs):
+                term = row * rec[w][v]
+                total[v] = term if w == 0 else total[v] + term
+    return [(total[0] + total[2], total[1] - total[0]) for total in sums]
+
+
+def receiver_tiles(rec_ref, windows, pair):
+    spans = [pl.ds(pl.multiple_of(pair * 16 + half * 8, 8), 8) for half in range(2)]
+    recs = [
+        [[rec_ref[w, v, span, :] for v in range(3)] for w in range(windows)] for span in spans
+    ]
+    return spans, recs
+
+
+def partial_kernel(sizes, first, last, *refs):
+    groups, z_parts, wins, chans, src_local = sizes
+    count = groups * z_parts
+    pick_ref, out_ref, src_ref, rec_ref = refs[count:]
+    windows = groups * wins
+    for k in range(first, last):
+        choose_rows(refs[:count], pick_ref, src_ref, rec_ref, sizes, k)
+
+        def one_pair(pair, carry):
+            spans, recs = receiver_tiles(rec_ref, windows, pair)
+
+            def one_source(s, inner):
+                for span, sums in zip(spans, cross_sums(src_ref, s, recs)):
+                    for p in range(2):
+                        out_ref[k - first, s, p, span, :] = sums[p]
+                return inner
+
+            return lax.fori_loop(0, src_local, one_source, carry, unroll=8)
+
+        lax.fori_loop(0, chans // 16, one_pair, 0)
+
+
+def final_kernel(sizes, firsts, *refs):
+    groups, z_parts, wins, chans, src_local = sizes
+    count = groups * z_parts
+    parts = len(firsts)
+    part_refs = refs[count : count + parts]
+    pick_ref, rate_ref, inv_ref, out_ref = refs[count + parts : count + parts + 4]
+    src_ref, rec_ref, stack_ref, stage_ref, sems = refs[count + parts + 4 :]
+    windows = groups * wins
+    pairs = chans // 16
+    for k in range(KB):
+        choose_rows(refs[:count], pick_ref, src_ref, rec_ref, sizes, k)
+        index = max(i for i in range(parts) if firsts[i] <= k)
+        part_ref, part_k = part_refs[index], k - firsts[index]
+
+        def one_pair(pair, carry):
+            spans, recs = receiver_tiles(rec_ref, windows, pair)
+
+            def one_source(s, inner):
+                sums = cross_sums(src_ref, s, recs)
+                row = pl.multiple_of((s * pairs + pair) * 16, 16)
+                for p in range(2):
+                    both = [
+                        (total[p] + part_ref[part_k, s, p, span, :]) * rate_ref[s, span, :]
+                        for total, span in zip(sums, spans)
+                    ]
+                    stack_ref[2 * k + p, pl.ds(row, 16), :] = jnp.concatenate(
+                        both, axis=0
+                    ).astype(jnp.bfloat16)
+                return inner
+
+            return lax.fori_loop(0, src_local, one_source, carry, unroll=8)
+
+        lax.fori_loop(0, pairs, one_pair, 0)
     scale = 1.0 / math.sqrt(BAND)
-    chunk = min(8, src_local // 2)
-    for first in range(0, src_local // 2, chunk):
-        span = chunk * tiles * 16
-        left = jnp.concatenate(
-            [stack_ref[j, first * tiles * 16 : first * tiles * 16 + span, :] for j in range(2 * KB)],
-            axis=1,
+    chunk = min(16, src_local)
+    copies = []
+    for index, first in enumerate(range(0, src_local, chunk)):
+        span = slice(first * chans, (first + chunk) * chans)
+        left = jnp.concatenate([stack_ref[j, span, :] for j in range(2 * KB)], axis=1)
+        summed = jnp.dot(left, inv_ref[...], preferred_element_type=jnp.float32) * scale
+        stage_ref[first : first + chunk] = summed.astype(jnp.bfloat16).reshape(chunk, chans, LAGS)
+        copies.append(
+            pltpu.make_async_copy(
+                stage_ref.at[pl.ds(first, chunk)], out_ref.at[pl.ds(first, chunk)], sems.at[index]
+            )
         )
-        summed = jnp.dot(left, inv_ref[...], preferred_element_type=jnp.float32) * scale
-        for i in range(chunk):
-            for half in range(2):
-                pieces = [
-                    summed[((i * tiles + t) * 2 + half) * 8 : ((i * tiles + t) * 2 + half + 1) * 8]
-                    for t in range(tiles)
-                ]
-                out_ref[2 * (first + i) + half] = jnp.concatenate(pieces, axis=0).astype(
-                    jnp.bfloat16
-                )
-
-
-def shifted(value, axis, distance):
+        copies[-1].start()
+    for copy in copies:
+        copy.wait()
+
+
+def held(values):
+    small = sum(v.size * v.dtype.itemsize for v in values) <= 24 * 2**20
+    return [pl.BlockSpec(memory_space=pltpu.VMEM) if small else pl.BlockSpec()] * len(values)
+
+
+def work_space(sizes):
+    groups, _, wins, chans, src_local = sizes
+    return [
+        pltpu.VMEM((groups * wins, 3, src_local, LANE), jnp.float32),
+        pltpu.VMEM((groups * wins, 3, chans, LANE), jnp.float32),
+    ]
+
+
+def partial_cross(sizes, blocks, pick, first, last):
+    chans, src_local = sizes[3:]
+    operands = (*blocks, pick)
+    return pl.pallas_call(
+        lambda *refs: partial_kernel(sizes, first, last, *refs),
+        in_specs=held(operands),
+        out_specs=pl.BlockSpec(memory_space=pltpu.VMEM),
+        out_shape=jax.ShapeDtypeStruct((last - first, src_local, 2, chans, LANE), jnp.float32),
+        scratch_shapes=work_space(sizes),
+        compiler_params=pltpu.CompilerParams(vmem_limit_bytes=LIMIT),
+    )(*operands)
+
+
+def final_cross(sizes, blocks, parts, firsts, pick, rate):
+    chans, src_local = sizes[3:]
+    operands = (*blocks, *parts, pick, rate, jnp.asarray(inverse_table()))
+    chunks = src_local // min(16, src_local)
+    return pl.pallas_call(
+        lambda *refs: final_kernel(sizes, firsts, *refs),
+        in_specs=held(operands),
+        out_specs=pl.BlockSpec(memory_space=pl.ANY),
+        out_shape=jax.ShapeDtypeStruct((src_local, chans, LAGS), jnp.bfloat16),
+        scratch_shapes=work_space(sizes)
+        + [
+            pltpu.VMEM((2 * KB, src_local * chans, LANE), jnp.bfloat16),
+            pltpu.VMEM((src_local, chans, LAGS), jnp.bfloat16),
+            pltpu.SemaphoreType.DMA((chunks,)),
+        ],
+        compiler_params=pltpu.CompilerParams(vmem_limit_bytes=LIMIT),
+        name="cross",
+    )(*operands)
+
+
+def exchanged(value, axis, distance):
     count = lax.axis_size(axis)
-    return lax.ppermute(value, axis, [(i, (i + distance) % count) for i in range(count)])
-
-
-def shards(traces, src_index, valid):
+    return lax.ppermute(value, axis, [(i, i ^ distance) for i in range(count)])
+
+
+def whole_step(traces, src_index, valid):
     win_count, chans, _ = traces.shape
     rx_count, tw_count, fq_count = (lax.axis_size(a) for a in ("rx", "tw", "fq"))
     rx_pos, tw_pos, fq_pos = (lax.axis_index(a) for a in ("rx", "tw", "fq"))
     wins = win_count // fq_count
     own = spectra(traces, fq_pos, fq_count)
 
-    along_z = [own] + [shifted(own, "rx", d) for d in range(1, rx_count)]
+    along_z = [own] + [exchanged(own, "rx", d) for d in range(1, rx_count)]
     if rx_count > 4:
         along_z = [jnp.concatenate(along_z, axis=0)]
-    groups = [along_z]
-    for d in range(1, tw_count):
-        groups.append([shifted(v, "tw", d) for v in along_z])
+    near = [along_z]
     for d in range(1, fq_count):
-        groups = groups + [[shifted(v, "fq", d) for v in g] for g in groups]
+        near.append([exchanged(v, "fq", d) for v in along_z])
+    far = []
+    for t in range(1, tw_count):
+        far.append([exchanged(v, "tw", t) for v in along_z])
+        for d in range(1, fq_count):
+            far.append([exchanged(v, "fq", d) for v in far[-1]])
     z_parts = len(along_z)
 
     valid_float = valid.astype(jnp.float32)
@@ -231,14 +319,14 @@
     own_rec = rx_pos * chans + jnp.arange(chans, dtype=jnp.int32)
     wanted = jnp.concatenate([own_src, own_rec])
     channel_ids = (
-        (rx_pos - jnp.arange(rx_count, dtype=jnp.int32)[:, None]) % rx_count * chans
+        (rx_pos ^ jnp.arange(rx_count, dtype=jnp.int32)[:, None]) * chans
         + jnp.arange(chans, dtype=jnp.int32)[None, :]
     ).reshape(-1)
     channel_total = rx_count * chans
     window_ids = []
-    for f in range(fq_count):
-        for t in range(tw_count):
-            block = (tw_pos - t) % tw_count * fq_count + (fq_pos - f) % fq_count
+    for t in range(tw_count):
+        for f in range(fq_count):
+            block = (tw_pos ^ t) * fq_count + (fq_pos ^ f)
             window_ids.append(block * wins + jnp.arange(wins, dtype=jnp.int32))
     window_ids = jnp.concatenate(window_ids)
     windows = window_ids.shape[0]
@@ -260,23 +348,21 @@
         (1.0 / jnp.maximum(pair_count, 1.0))[:, :, None], (src_local, chans, LANE)
     )
 
-    operands = [v for g in groups for v in g]
-    sizes = (len(groups), z_parts, wins, chans, src_local)
-    return pl.pallas_call(
-        lambda *refs: cross_kernel(sizes, *refs),
-        out_shape=jax.ShapeDtypeStruct((src_local, chans, LAGS), jnp.bfloat16),
-        scratch_shapes=[
-            pltpu.VMEM((windows, KB, 3, src_local, LANE), jnp.float32),
-            pltpu.VMEM((windows, KB, 3, chans, LANE), jnp.float32),
-            pltpu.VMEM((2 * KB, src_local * chans, LANE), jnp.bfloat16),
-        ],
-        name="cross",
-    )(*operands, pick, rate, jnp.asarray(inverse_table()))
+    near_windows = len(near) * wins
+    sizes = (len(near), z_parts, wins, chans, src_local)
+    near_blocks = [v for g in near for v in g]
+    firsts = (0, SPLIT)
+    parts = []
+    for first, last in zip(firsts, (*firsts[1:], KB)):
+        parts.append(partial_cross(sizes, near_blocks, pick[:near_windows], first, last))
+    sizes = (len(far), z_parts, wins, chans, src_local)
+    far_blocks = [v for g in far for v in g]
+    return final_cross(sizes, far_blocks, parts, firsts, pick[near_windows:], rate)
 
 
 def solution(mesh):
     return jax.shard_map(
-        shards,
+        whole_step,
         mesh=mesh,
         in_specs=(P("tw", ("grp", "rx"), None), P("grp", None), P(None, "grp")),
         out_specs=P(("tw", "fq"), ("grp", "rx"), None),

time: 52.3 us -> 46 us (0.88)
  Pallas kernels: 22.9 us -> 18.6 us
  waiting for transfers between devices: 14.5 us -> 12.5 us
  starting transfers between devices: 11 us -> 11.8 us
  other arithmetic: 1.17 us -> 0.5 us
    pallas_call x1 -> x3, Pallas kernels: 17.1 us -> 12.8 us  [the longest x1 8.38 us: final_cross(): pl.pallas_call(lambda *refs: final_kernel(sizes, firsts, *refs), in_specs...]
    ppermute x15, waiting for transfers between devices: 14.5 us -> 12.5 us  [exchanged(): return lax.ppermute(value, axis, [(i, i ^ distance) for i in range(count)])]
    broadcast_in_dim x1, local copies, waits for them, and re-layouts: 1.31 us -> 0.33 us  [whole_step(): jnp.broadcast_to((1.0 / jnp.maximum(pair_count, 1.0))[:, :, None], (src_l...]
    unnamed x34 -> x10, local copies, waits for them, and re-layouts: 0.07 us -> 0.92 us
    ppermute x15, starting transfers between devices: 11 us -> 11.8 us  [exchanged(): return lax.ppermute(value, axis, [(i, i ^ distance) for i in range(count)])]
    convert_element_type x1, other arithmetic: 0.85 us -> 0.16 us  [whole_step(): pick = jnp.where(wanted[None, :, None] == channel_ids[None, None, :], use...]
  transfers between devices with their start and end apart: 15 -> 15, of which waited for: 5 -> 4; matrix products, arithmetic and copies ran while one was open for 4% -> 3% of each run, Pallas kernels for 0% -> 10%
where the time goes in v2:
time: 46 us; the launch traced here: 45.8 us
  Pallas kernels  18.6 us (40%)
  waiting for transfers between devices  12.5 us (27%)
  starting transfers between devices  11.8 us (26%)
  local copies, waits for them, and re-layouts  1.59 us (3%)
  matrix products  0.55 us (1%)
  other arithmetic  0.5 us (1%)
    ppermute x15, waiting for transfers between devices, exchanged(): return lax.ppermute(value, axis, [(i, i ^ distance) for i in range(count)])  12.5 us
    ppermute x15, starting transfers between devices, exchanged(): return lax.ppermute(value, axis, [(i, i ^ distance) for i in range(count)])  11.8 us
    pallas_call x1, Pallas kernels, final_cross(): pl.pallas_call(lambda *refs: final_kernel(sizes, firsts, *refs), in_specs...  8.38 us
    pallas_call x1, Pallas kernels, spectra(): pl.pallas_call(spectra_kernel, grid_spec=grid_spec, out_shape=jax.ShapeDt...  5.87 us
    pallas_call x2, Pallas kernels, partial_cross(): pl.pallas_call(lambda *refs: partial_kernel(sizes, first, last, *refs), i...  4.38 us
  transfers between devices with their start and end apart: 15, of which 4 were waited for; matrix products, arithmetic and copies ran while one was open for 3% of the time, Pallas kernels for 10%

profile of v2, /device:TPU:0, one launch (start us, length us, event | category | flops | bytes accessed | tf_op | source)
XLA Modules:
  0.0 45.8 jit_solution(17430431109594129932)
XLA Ops:
  0.0 5.9 %spectra.1.refs_0_ = bf16[2,32,1024]{2,1,0:T(8,128)(2,1)} custom-call(s32[1]{0:T(128)} %bitcast.pos_ref, bf16[4,32,15360]{2,1,0:T(8,128)(2,1)} %trace_ref.1, bf16[1024,1024]{1,0:T(8,128)(2,1)} %constant.34.clone.coef_ref, f32[15,1024]{1,0:T(8,128)} %constant.35.clone.turn_ref), custom_call_target="tpu_custom_call" | custom-call | tf_op jit(solution)/shard_map/spectra/pallas_call | solution.py:118
  5.9 0.5 %collective-permute-start.11 = (bf16[2,32,1024]{2,1,0:T(8,128)(2,1)}, bf16[2,32,1024]{2,1,0:T(8,128)(2,1)S(1)}, u32[]{:S(2)}, u32[]{:S(2)}) collective-permute-start(bf16[2,32,1024]{2,1,0:T(8,128)(2,1)} %spectra.1.refs_0_), channel_id=1, source_target_pairs={{0,1},{1,0},{2,3},{3,2},{4,5},{5,4},{6,7},{7,6},{8,9},{9,8},{10,11... | collective-permute-start | bytes 393224 | tf_op jit(solution)/shard_map/ppermute | solution.py:291
  6.4 4.6 %collective-permute-start.5 = (bf16[2,32,1024]{2,1,0:T(8,128)(2,1)}, bf16[2,32,1024]{2,1,0:T(8,128)(2,1)S(1)}, u32[]{:S(2)}, u32[]{:S(2)}) collective-permute-start(bf16[2,32,1024]{2,1,0:T(8,128)(2,1)} %spectra.1.refs_0_), channel_id=1, source_target_pairs={{0,12},{4,8},{8,4},{12,0},{1,13},{5,9},{9,5},{13,1},{2,14},{6,10},... | collective-permute-start | bytes 393224 | tf_op jit(solution)/shard_map/ppermute | solution.py:291
  11.0 0.0 collective-permute-start.3
  11.0 0.6 %collective-permute-start.1 = (bf16[2,32,1024]{2,1,0:T(8,128)(2,1)}, bf16[2,32,1024]{2,1,0:T(8,128)(2,1)S(1)}, u32[]{:S(2)}, u32[]{:S(2)}) collective-permute-start(bf16[2,32,1024]{2,1,0:T(8,128)(2,1)} %spectra.1.refs_0_), channel_id=1, source_target_pairs={{0,4},{4,0},{8,12},{12,8},{1,5},{5,1},{9,13},{13,9},{2,6},{6,2},{1... | collective-permute-start | bytes 393224 | tf_op jit(solution)/shard_map/ppermute | solution.py:291
  11.7 1.6 %collective-permute-start = (bf16[2,32,1024]{2,1,0:T(8,128)(2,1)}, bf16[2,32,1024]{2,1,0:T(8,128)(2,1)S(1)}, u32[]{:S(2)}, u32[]{:S(2)}) collective-permute-start(bf16[2,32,1024]{2,1,0:T(8,128)(2,1)} %spectra.1.refs_0_), channel_id=1, source_target_pairs={{0,2},{2,0},{1,3},{3,1},{4,6},{6,4},{5,7},{7,5},{8,10},{10,8},{9,1... | collective-permute-start | bytes 393224 | tf_op jit(solution)/shard_map/ppermute | solution.py:291
  13.3 0.1 reshape.63
  13.4 0.1 iota_add_fusion
  13.5 0.1 add.73
  13.6 0.1 dynamic_slice.3
  13.6 0.1 pad_add_fusion
  13.7 0.1 pad_add_fusion.1
  13.8 0.3 fusion.1
  14.1 0.3 fusion
  14.3 0.1 copy.7
  14.4 0.1 broadcast_compare_fusion
  14.5 1.1 %collective-permute-done.5.refs_3_ = bf16[2,32,1024]{2,1,0:T(8,128)(2,1)S(1)} collective-permute-done((bf16[2,32,1024]{2,1,0:T(8,128)(2,1)}, bf16[2,32,1024]{2,1,0:T(8,128)(2,1)S(1)}, u32[]{:S(2)}, u32[]{:S(2)}) %collective-permute-start.5) | collective-permute-done | bytes 131104 | tf_op jit(solution)/shard_map/ppermute | solution.py:291
  15.7 0.0 collective-permute-start.14
  15.7 0.0 collective-permute-done.11.refs_4_
  15.7 1.7 %collective-permute-start.6 = (bf16[2,32,1024]{2,1,0:T(8,128)(2,1)S(1)}, bf16[2,32,1024]{2,1,0:T(8,128)(2,1)S(1)}, u32[]{:S(2)}, u32[]{:S(2)}) collective-permute-start(bf16[2,32,1024]{2,1,0:T(8,128)(2,1)S(1)} %collective-permute-done.5.refs_3_), channel_id=1, source_target_pairs={{0,2},{2,0},{1,3},{3,1},{4,6},{6,4},{5,7},{7,5},{8,10},{10,8},{9,1... | collective-permute-start | bytes 393224 | tf_op jit(solution)/shard_map/ppermute | solution.py:291
  17.4 5.5 %collective-permute-done.3.refs_2_ = bf16[2,32,1024]{2,1,0:T(8,128)(2,1)S(1)} collective-permute-done((bf16[2,32,1024]{2,1,0:T(8,128)(2,1)}, bf16[2,32,1024]{2,1,0:T(8,128)(2,1)S(1)}, u32[]{:S(2)}, u32[]{:S(2)}) %collective-permute-start.3) | collective-permute-done | bytes 131104 | tf_op jit(solution)/shard_map/ppermute | solution.py:291
  22.9 0.0 collective-permute-start.13
  22.9 0.0 collective-permute-done.1.refs_1_
  22.9 1.5 %collective-permute-start.4 = (bf16[2,32,1024]{2,1,0:T(8,128)(2,1)S(1)}, bf16[2,32,1024]{2,1,0:T(8,128)(2,1)S(1)}, u32[]{:S(2)}, u32[]{:S(2)}) collective-permute-start(bf16[2,32,1024]{2,1,0:T(8,128)(2,1)S(1)} %collective-permute-done.3.refs_2_), channel_id=1, source_target_pairs={{0,2},{2,0},{1,3},{3,1},{4,6},{6,4},{5,7},{7,5},{8,10},{10,8},{9,1... | collective-permute-start | bytes 393224 | tf_op jit(solution)/shard_map/ppermute | solution.py:291
  24.4 0.0 collective-permute-done.refs_0_
  24.4 0.5 %collective-permute-start.2 = (bf16[2,32,1024]{2,1,0:T(8,128)(2,1)S(1)}, bf16[2,32,1024]{2,1,0:T(8,128)(2,1)S(1)}, u32[]{:S(2)}, u32[]{:S(2)}) collective-permute-start(bf16[2,32,1024]{2,1,0:T(8,128)(2,1)S(1)} %collective-permute-done.1.refs_1_), channel_id=1, source_target_pairs={{0,2},{2,0},{1,3},{3,1},{4,6},{6,4},{5,7},{7,5},{8,10},{10,8},{9,1... | collective-permute-start | bytes 393224 | tf_op jit(solution)/shard_map/ppermute | solution.py:291
  25.0 0.2 select_convert_fusion
  25.1 0.0 collective-permute-done.14.refs_7_
  25.1 0.1 collective-permute-start.12
  25.2 0.0 collective-permute-done.6.refs_3_
  25.2 0.5 %collective-permute-start.7 = (bf16[2,32,1024]{2,1,0:T(8,128)(2,1)S(1)}, bf16[2,32,1024]{2,1,0:T(8,128)(2,1)S(1)}, u32[]{:S(2)}, u32[]{:S(2)}) collective-permute-start(bf16[2,32,1024]{2,1,0:T(8,128)(2,1)S(1)} %collective-permute-done.refs_0_), channel_id=1, source_target_pairs={{0,1},{1,0},{2,3},{3,2},{4,5},{5,4},{6,7},{7,6},{8,9},{9,8},{10,11... | collective-permute-start | bytes 393224 | tf_op jit(solution)/shard_map/ppermute | solution.py:291
  25.7 0.0 collective-permute-done.13.refs_6_
  25.7 0.1 collective-permute-start.10
  25.8 3.5 %collective-permute-done.4.refs_2_ = bf16[2,32,1024]{2,1,0:T(8,128)(2,1)S(1)} collective-permute-done((bf16[2,32,1024]{2,1,0:T(8,128)(2,1)S(1)}, bf16[2,32,1024]{2,1,0:T(8,128)(2,1)S(1)}, u32[]{:S(2)}, u32[]{:S(2)}) %collective-permute-start.4) | collective-permute-done | bytes 131104 | tf_op jit(solution)/shard_map/ppermute | solution.py:291
  29.3 0.0 collective-permute-start.9
  29.3 2.3 %collective-permute-done.2.refs_1_ = bf16[2,32,1024]{2,1,0:T(8,128)(2,1)S(1)} collective-permute-done((bf16[2,32,1024]{2,1,0:T(8,128)(2,1)S(1)}, bf16[2,32,1024]{2,1,0:T(8,128)(2,1)S(1)}, u32[]{:S(2)}, u32[]{:S(2)}) %collective-permute-start.2) | collective-permute-done | bytes 131104 | tf_op jit(solution)/shard_map/ppermute | solution.py:291
  31.6 0.0 collective-permute-start.8
  31.7 0.0 collective-permute-done.12.refs_5_
  31.7 0.0 copy-start
  31.7 0.9 %copy-done = bf16[2,32,1024]{2,1,0:T(8,128)(2,1)S(1)} copy-done((bf16[2,32,1024]{2,1,0:T(8,128)(2,1)S(1)}, bf16[2,32,1024]{2,1,0:T(8,128)(2,1)}, u32[]{:S(2)}) %copy-start) | copy-done | bytes 131096
  32.6 2.2 %shard_map.65.refs_9_ = f32[2,64,2,32,128]{4,3,2,1,0:T(8,128)S(1)} custom-call(bf16[2,32,1024]{2,1,0:T(8,128)(2,1)S(1)} %copy-done, bf16[2,32,1024]{2,1,0:T(8,128)(2,1)S(1)} %collective-permute-done.1.refs_1_, bf16[2,32,1024]{2,1,0:T(8,128)(2,1)S(1)} %collective-permute-done.3.refs_2_, bf16[2,32,1024]{2,1,0:T(8,128)(2,1)S(1)} %collective-permute-done.5.refs_3_, ...), custom_call_target="tpu_custom_call" | custom-call | tf_op jit(solution)/shard_map/pallas_call | solution.py:259
  34.8 0.0 copy-start.2
  34.8 2.2 %shard_map.64.refs_8_ = f32[2,64,2,32,128]{4,3,2,1,0:T(8,128)S(1)} custom-call(bf16[2,32,1024]{2,1,0:T(8,128)(2,1)S(1)} %copy-done.1, bf16[2,32,1024]{2,1,0:T(8,128)(2,1)S(1)} %collective-permute-done.1.refs_1_, bf16[2,32,1024]{2,1,0:T(8,128)(2,1)S(1)} %collective-permute-done.3.refs_2_, bf16[2,32,1024]{2,1,0:T(8,128)(2,1)S(1)} %collective-permute-done.5.refs_3_, ...), custom_call_target="tpu_custom_call" | custom-call | tf_op jit(solution)/shard_map/pallas_call | solution.py:259
  37.0 0.0 collective-permute-done.7.refs_4_
  37.0 0.0 collective-permute-done.10.refs_7_
  37.0 0.0 collective-permute-done.9.refs_6_
  37.0 0.3 broadcast_in_dim.25.refs_11_
  37.4 8.4 %cross.1 = bf16[64,32,512]{2,1,0:T(8,128)(2,1)} custom-call(bf16[2,32,1024]{2,1,0:T(8,128)(2,1)S(1)} %collective-permute-done.refs_0_, bf16[2,32,1024]{2,1,0:T(8,128)(2,1)S(1)} %collective-permute-done.2.refs_1_, bf16[2,32,1024]{2,1,0:T(8,128)(2,1)S(1)} %collective-permute-done.4.refs_2_, bf16[2,32,1024]{2,1,0:T(8,128)(2,1)S(1)} %collective-permute-done.6.refs_3_, ...), custom_call_target="tpu_custom_call" | custom-call | tf_op jit(solution)/shard_map/cross/pallas_call | solution.py:273
  (13 shorter events, 0.0 us)
Async XLA Ops:
  0.0 13.3 %copy-start.3 = (s32[4,64]{1,0:T(4,128)S(1)}, s32[4,64]{1,0:T(4,128)}, u32[]{:S(2)}) copy-start(s32[4,64]{1,0:T(4,128)} %param.7) | copy-start | bytes 3076
  0.0 13.8 %copy-start.4 = (s32[8,128]{1,0:T(8,128)S(1)}, s32[8,128]{1,0:T(8,128)}, u32[]{:S(2)}) copy-start(s32[8,128]{1,0:T(8,128)} %param.8) | copy-start | bytes 12292
  5.9 28.9 %copy-start.1 = (bf16[2,32,1024]{2,1,0:T(8,128)(2,1)S(1)}, bf16[2,32,1024]{2,1,0:T(8,128)(2,1)}, u32[]{:S(2)}) copy-start(bf16[2,32,1024]{2,1,0:T(8,128)(2,1)} %spectra.1.refs_0_) | copy-start | bytes 393220
  5.9 9.8 %collective-permute-start.11 = (bf16[2,32,1024]{2,1,0:T(8,128)(2,1)}, bf16[2,32,1024]{2,1,0:T(8,128)(2,1)S(1)}, u32[]{:S(2)}, u32[]{:S(2)}) collective-permute-start(bf16[2,32,1024]{2,1,0:T(8,128)(2,1)} %spectra.1.refs_0_), channel_id=1, source_target_pairs={{0,1},{1,0},{2,3},{3,2},{4,5},{5,4},{6,7},{7,6},{8,9},{9,8},{10,11... | collective-permute-start | bytes 393224 | tf_op jit(solution)/shard_map/ppermute | solution.py:291
  6.4 9.3 %collective-permute-start.5 = (bf16[2,32,1024]{2,1,0:T(8,128)(2,1)}, bf16[2,32,1024]{2,1,0:T(8,128)(2,1)S(1)}, u32[]{:S(2)}, u32[]{:S(2)}) collective-permute-start(bf16[2,32,1024]{2,1,0:T(8,128)(2,1)} %spectra.1.refs_0_), channel_id=1, source_target_pairs={{0,12},{4,8},{8,4},{12,0},{1,13},{5,9},{9,5},{13,1},{2,14},{6,10},... | collective-permute-start | bytes 393224 | tf_op jit(solution)/shard_map/ppermute | solution.py:291
  11.0 11.9 %collective-permute-start.3 = (bf16[2,32,1024]{2,1,0:T(8,128)(2,1)}, bf16[2,32,1024]{2,1,0:T(8,128)(2,1)S(1)}, u32[]{:S(2)}, u32[]{:S(2)}) collective-permute-start(bf16[2,32,1024]{2,1,0:T(8,128)(2,1)} %spectra.1.refs_0_), channel_id=1, source_target_pairs={{0,8},{4,12},{8,0},{12,4},{1,9},{5,13},{9,1},{13,5},{2,10},{6,14},... | collective-permute-start | bytes 393224 | tf_op jit(solution)/shard_map/ppermute | solution.py:291
  11.0 11.9 %collective-permute-start.1 = (bf16[2,32,1024]{2,1,0:T(8,128)(2,1)}, bf16[2,32,1024]{2,1,0:T(8,128)(2,1)S(1)}, u32[]{:S(2)}, u32[]{:S(2)}) collective-permute-start(bf16[2,32,1024]{2,1,0:T(8,128)(2,1)} %spectra.1.refs_0_), channel_id=1, source_target_pairs={{0,4},{4,0},{8,12},{12,8},{1,5},{5,1},{9,13},{13,9},{2,6},{6,2},{1... | collective-permute-start | bytes 393224 | tf_op jit(solution)/shard_map/ppermute | solution.py:291
  11.7 12.8 %collective-permute-start = (bf16[2,32,1024]{2,1,0:T(8,128)(2,1)}, bf16[2,32,1024]{2,1,0:T(8,128)(2,1)S(1)}, u32[]{:S(2)}, u32[]{:S(2)}) collective-permute-start(bf16[2,32,1024]{2,1,0:T(8,128)(2,1)} %spectra.1.refs_0_), channel_id=1, source_target_pairs={{0,2},{2,0},{1,3},{3,1},{4,6},{6,4},{5,7},{7,5},{8,10},{10,8},{9,1... | collective-permute-start | bytes 393224 | tf_op jit(solution)/shard_map/ppermute | solution.py:291
  15.7 9.4 %collective-permute-start.14 = (bf16[2,32,1024]{2,1,0:T(8,128)(2,1)S(1)}, bf16[2,32,1024]{2,1,0:T(8,128)(2,1)S(1)}, u32[]{:S(2)}, u32[]{:S(2)}) collective-permute-start(bf16[2,32,1024]{2,1,0:T(8,128)(2,1)S(1)} %collective-permute-done.5.refs_3_), channel_id=1, source_target_pairs={{0,1},{1,0},{2,3},{3,2},{4,5},{5,4},{6,7},{7,6},{8,9},{9,8},{10,11... | collective-permute-start | bytes 393224 | tf_op jit(solution)/shard_map/ppermute | solution.py:291
  15.7 9.5 %collective-permute-start.6 = (bf16[2,32,1024]{2,1,0:T(8,128)(2,1)S(1)}, bf16[2,32,1024]{2,1,0:T(8,128)(2,1)S(1)}, u32[]{:S(2)}, u32[]{:S(2)}) collective-permute-start(bf16[2,32,1024]{2,1,0:T(8,128)(2,1)S(1)} %collective-permute-done.5.refs_3_), channel_id=1, source_target_pairs={{0,2},{2,0},{1,3},{3,1},{4,6},{6,4},{5,7},{7,5},{8,10},{10,8},{9,1... | collective-permute-start | bytes 393224 | tf_op jit(solution)/shard_map/ppermute | solution.py:291
  22.9 2.8 %collective-permute-start.13 = (bf16[2,32,1024]{2,1,0:T(8,128)(2,1)S(1)}, bf16[2,32,1024]{2,1,0:T(8,128)(2,1)S(1)}, u32[]{:S(2)}, u32[]{:S(2)}) collective-permute-start(bf16[2,32,1024]{2,1,0:T(8,128)(2,1)S(1)} %collective-permute-done.3.refs_2_), channel_id=1, source_target_pairs={{0,1},{1,0},{2,3},{3,2},{4,5},{5,4},{6,7},{7,6},{8,9},{9,8},{10,11... | collective-permute-start | bytes 393224 | tf_op jit(solution)/shard_map/ppermute | solution.py:291
  22.9 6.4 %collective-permute-start.4 = (bf16[2,32,1024]{2,1,0:T(8,128)(2,1)S(1)}, bf16[2,32,1024]{2,1,0:T(8,128)(2,1)S(1)}, u32[]{:S(2)}, u32[]{:S(2)}) collective-permute-start(bf16[2,32,1024]{2,1,0:T(8,128)(2,1)S(1)} %collective-permute-done.3.refs_2_), channel_id=1, source_target_pairs={{0,2},{2,0},{1,3},{3,1},{4,6},{6,4},{5,7},{7,5},{8,10},{10,8},{9,1... | collective-permute-start | bytes 393224 | tf_op jit(solution)/shard_map/ppermute | solution.py:291
  24.4 7.2 %collective-permute-start.2 = (bf16[2,32,1024]{2,1,0:T(8,128)(2,1)S(1)}, bf16[2,32,1024]{2,1,0:T(8,128)(2,1)S(1)}, u32[]{:S(2)}, u32[]{:S(2)}) collective-permute-start(bf16[2,32,1024]{2,1,0:T(8,128)(2,1)S(1)} %collective-permute-done.1.refs_1_), channel_id=1, source_target_pairs={{0,2},{2,0},{1,3},{3,1},{4,6},{6,4},{5,7},{7,5},{8,10},{10,8},{9,1... | collective-permute-start | bytes 393224 | tf_op jit(solution)/shard_map/ppermute | solution.py:291
  25.1 6.5 %collective-permute-start.12 = (bf16[2,32,1024]{2,1,0:T(8,128)(2,1)S(1)}, bf16[2,32,1024]{2,1,0:T(8,128)(2,1)S(1)}, u32[]{:S(2)}, u32[]{:S(2)}) collective-permute-start(bf16[2,32,1024]{2,1,0:T(8,128)(2,1)S(1)} %collective-permute-done.1.refs_1_), channel_id=1, source_target_pairs={{0,1},{1,0},{2,3},{3,2},{4,5},{5,4},{6,7},{7,6},{8,9},{9,8},{10,11... | collective-permute-start | bytes 393224 | tf_op jit(solution)/shard_map/ppermute | solution.py:291
  25.2 11.8 %collective-permute-start.7 = (bf16[2,32,1024]{2,1,0:T(8,128)(2,1)S(1)}, bf16[2,32,1024]{2,1,0:T(8,128)(2,1)S(1)}, u32[]{:S(2)}, u32[]{:S(2)}) collective-permute-start(bf16[2,32,1024]{2,1,0:T(8,128)(2,1)S(1)} %collective-permute-done.refs_0_), channel_id=1, source_target_pairs={{0,1},{1,0},{2,3},{3,2},{4,5},{5,4},{6,7},{7,6},{8,9},{9,8},{10,11... | collective-permute-start | bytes 393224 | tf_op jit(solution)/shard_map/ppermute | solution.py:291
  25.7 11.3 %collective-permute-start.10 = (bf16[2,32,1024]{2,1,0:T(8,128)(2,1)S(1)}, bf16[2,32,1024]{2,1,0:T(8,128)(2,1)S(1)}, u32[]{:S(2)}, u32[]{:S(2)}) collective-permute-start(bf16[2,32,1024]{2,1,0:T(8,128)(2,1)S(1)} %collective-permute-done.6.refs_3_), channel_id=1, source_target_pairs={{0,1},{1,0},{2,3},{3,2},{4,5},{5,4},{6,7},{7,6},{8,9},{9,8},{10,11... | collective-permute-start | bytes 393224 | tf_op jit(solution)/shard_map/ppermute | solution.py:291
  29.3 7.7 %collective-permute-start.9 = (bf16[2,32,1024]{2,1,0:T(8,128)(2,1)S(1)}, bf16[2,32,1024]{2,1,0:T(8,128)(2,1)S(1)}, u32[]{:S(2)}, u32[]{:S(2)}) collective-permute-start(bf16[2,32,1024]{2,1,0:T(8,128)(2,1)S(1)} %collective-permute-done.4.refs_2_), channel_id=1, source_target_pairs={{0,1},{1,0},{2,3},{3,2},{4,5},{5,4},{6,7},{7,6},{8,9},{9,8},{10,11... | collective-permute-start | bytes 393224 | tf_op jit(solution)/shard_map/ppermute | solution.py:291
  31.6 5.4 %collective-permute-start.8 = (bf16[2,32,1024]{2,1,0:T(8,128)(2,1)S(1)}, bf16[2,32,1024]{2,1,0:T(8,128)(2,1)S(1)}, u32[]{:S(2)}, u32[]{:S(2)}) collective-permute-start(bf16[2,32,1024]{2,1,0:T(8,128)(2,1)S(1)} %collective-permute-done.2.refs_1_), channel_id=1, source_target_pairs={{0,1},{1,0},{2,3},{3,2},{4,5},{5,4},{6,7},{7,6},{8,9},{9,8},{10,11... | collective-permute-start | bytes 393224 | tf_op jit(solution)/shard_map/ppermute | solution.py:291
  31.7 0.9 %copy-start = (bf16[2,32,1024]{2,1,0:T(8,128)(2,1)S(1)}, bf16[2,32,1024]{2,1,0:T(8,128)(2,1)}, u32[]{:S(2)}) copy-start(bf16[2,32,1024]{2,1,0:T(8,128)(2,1)} %spectra.1.refs_0_) | copy-start | bytes 393220
  34.8 2.6 %copy-start.2 = (bf16[1024,512]{1,0:T(8,128)(2,1)S(1)}, bf16[1024,512]{1,0:T(8,128)(2,1)}, u32[]{:S(2)}) copy-start(bf16[1024,512]{1,0:T(8,128)(2,1)} %constant.36.clone.refs_12_) | copy-start | bytes 3145732

commit v3 on v2

--- a/solution.py
+++ b/solution.py
@@ -17,7 +17,6 @@
 LANE = 128
 KB = BAND // LANE
 SPLIT = 2
-LIMIT = 40 * 2**20
 EPS = 1e-05
 
 
@@ -184,7 +183,7 @@
                         out_ref[k - first, s, p, span, :] = sums[p]
                 return inner
 
-            return lax.fori_loop(0, src_local, one_source, carry, unroll=8)
+            return lax.fori_loop(0, src_local, one_source, carry, unroll=16)
 
         lax.fori_loop(0, chans // 16, one_pair, 0)
 
@@ -219,7 +218,7 @@
                     ).astype(jnp.bfloat16)
                 return inner
 
-            return lax.fori_loop(0, src_local, one_source, carry, unroll=8)
+            return lax.fori_loop(0, src_local, one_source, carry, unroll=16)
 
         lax.fori_loop(0, pairs, one_pair, 0)
     scale = 1.0 / math.sqrt(BAND)
@@ -241,8 +240,9 @@
 
 
 def held(values):
-    small = sum(v.size * v.dtype.itemsize for v in values) <= 24 * 2**20
-    return [pl.BlockSpec(memory_space=pltpu.VMEM) if small else pl.BlockSpec()] * len(values)
+    small = sum(v.size * v.dtype.itemsize for v in values) <= 16 * 2**20
+    specs = [pl.BlockSpec(memory_space=pltpu.VMEM) if small else pl.BlockSpec()] * len(values)
+    return specs, pltpu.CompilerParams(vmem_limit_bytes=(16 if small else 48) * 2**20)
 
 
 def work_space(sizes):
@@ -256,13 +256,14 @@
 def partial_cross(sizes, blocks, pick, first, last):
     chans, src_local = sizes[3:]
     operands = (*blocks, pick)
+    specs, params = held(operands)
     return pl.pallas_call(
         lambda *refs: partial_kernel(sizes, first, last, *refs),
-        in_specs=held(operands),
+        in_specs=specs,
         out_specs=pl.BlockSpec(memory_space=pltpu.VMEM),
         out_shape=jax.ShapeDtypeStruct((last - first, src_local, 2, chans, LANE), jnp.float32),
         scratch_shapes=work_space(sizes),
-        compiler_params=pltpu.CompilerParams(vmem_limit_bytes=LIMIT),
+        compiler_params=params,
     )(*operands)
 
 
@@ -270,9 +271,10 @@
     chans, src_local = sizes[3:]
     operands = (*blocks, *parts, pick, rate, jnp.asarray(inverse_table()))
     chunks = src_local // min(16, src_local)
+    specs, params = held(operands)
     return pl.pallas_call(
         lambda *refs: final_kernel(sizes, firsts, *refs),
-        in_specs=held(operands),
+        in_specs=specs,
         out_specs=pl.BlockSpec(memory_space=pl.ANY),
         out_shape=jax.ShapeDtypeStruct((src_local, chans, LAGS), jnp.bfloat16),
         scratch_shapes=work_space(sizes)
@@ -281,7 +283,7 @@
             pltpu.VMEM((src_local, chans, LAGS), jnp.bfloat16),
             pltpu.SemaphoreType.DMA((chunks,)),
         ],
-        compiler_params=pltpu.CompilerParams(vmem_limit_bytes=LIMIT),
+        compiler_params=params,
         name="cross",
     )(*operands)
 
@@ -348,6 +350,7 @@
         (1.0 / jnp.maximum(pair_count, 1.0))[:, :, None], (src_local, chans, LANE)
     )
 
+    pick, rate = lax.optimization_barrier((pick, rate))
     near_windows = len(near) * wins
     sizes = (len(near), z_parts, wins, chans, src_local)
     near_blocks = [v for g in near for v in g]

time: 46 us -> 45.1 us (0.980)
  Pallas kernels: 18.6 us -> 18.1 us
  transfers between devices with their start and end apart: 15 -> 15, of which waited for: 4 -> 4; matrix products, arithmetic and copies ran while one was open for 3% -> 4% of each run, Pallas kernels for 10% -> 9%
where the time goes in v3:
time: 45.1 us; the launch traced here: 44.9 us
  Pallas kernels  18.1 us (40%)
  waiting for transfers between devices  12.2 us (27%)
  starting transfers between devices  11.8 us (26%)
  local copies, waits for them, and re-layouts  1.59 us (4%)
  matrix products  0.55 us (1%)
  other arithmetic  0.5 us (1%)
    ppermute x15, waiting for transfers between devices, exchanged(): return lax.ppermute(value, axis, [(i, i ^ distance) for i in range(count)])  12.2 us
    ppermute x15, starting transfers between devices, exchanged(): return lax.ppermute(value, axis, [(i, i ^ distance) for i in range(count)])  11.8 us
    pallas_call x1, Pallas kernels, final_cross(): pl.pallas_call(lambda *refs: final_kernel(sizes, firsts, *refs), in_specs...  8.02 us
    pallas_call x1, Pallas kernels, spectra(): pl.pallas_call(spectra_kernel, grid_spec=grid_spec, out_shape=jax.ShapeDt...  5.87 us
    pallas_call x2, Pallas kernels, partial_cross(): pl.pallas_call(lambda *refs: partial_kernel(sizes, first, last, *refs), i...  4.18 us
    unnamed x10, local copies, waits for them, and re-layouts  0.92 us
  transfers between devices with their start and end apart: 15, of which 4 were waited for; matrix products, arithmetic and copies ran while one was open for 4% of the time, Pallas kernels for 9%

profile of v3, /device:TPU:0, one launch (start us, length us, event | category | flops | bytes accessed | tf_op | source)
XLA Modules:
  0.0 44.9 jit_solution(17294994378411703842)
XLA Ops:
  0.0 5.9 %spectra.1.refs_0_ = bf16[2,32,1024]{2,1,0:T(8,128)(2,1)} custom-call(s32[1]{0:T(128)} %bitcast.pos_ref, bf16[4,32,15360]{2,1,0:T(8,128)(2,1)} %trace_ref.1, bf16[1024,1024]{1,0:T(8,128)(2,1)} %constant.34.clone.coef_ref, f32[15,1024]{1,0:T(8,128)} %constant.35.clone.turn_ref), custom_call_target="tpu_custom_call" | custom-call | tf_op jit(solution)/shard_map/spectra/pallas_call | solution.py:117
  5.9 0.5 %collective-permute-start.11 = (bf16[2,32,1024]{2,1,0:T(8,128)(2,1)}, bf16[2,32,1024]{2,1,0:T(8,128)(2,1)S(1)}, u32[]{:S(2)}, u32[]{:S(2)}) collective-permute-start(bf16[2,32,1024]{2,1,0:T(8,128)(2,1)} %spectra.1.refs_0_), channel_id=1, source_target_pairs={{0,1},{1,0},{2,3},{3,2},{4,5},{5,4},{6,7},{7,6},{8,9},{9,8},{10,11... | collective-permute-start | bytes 393224 | tf_op jit(solution)/shard_map/ppermute | solution.py:293
  6.4 4.6 %collective-permute-start.5 = (bf16[2,32,1024]{2,1,0:T(8,128)(2,1)}, bf16[2,32,1024]{2,1,0:T(8,128)(2,1)S(1)}, u32[]{:S(2)}, u32[]{:S(2)}) collective-permute-start(bf16[2,32,1024]{2,1,0:T(8,128)(2,1)} %spectra.1.refs_0_), channel_id=1, source_target_pairs={{0,12},{4,8},{8,4},{12,0},{1,13},{5,9},{9,5},{13,1},{2,14},{6,10},... | collective-permute-start | bytes 393224 | tf_op jit(solution)/shard_map/ppermute | solution.py:293
  11.0 0.0 collective-permute-start.3
  11.0 0.6 %collective-permute-start.1 = (bf16[2,32,1024]{2,1,0:T(8,128)(2,1)}, bf16[2,32,1024]{2,1,0:T(8,128)(2,1)S(1)}, u32[]{:S(2)}, u32[]{:S(2)}) collective-permute-start(bf16[2,32,1024]{2,1,0:T(8,128)(2,1)} %spectra.1.refs_0_), channel_id=1, source_target_pairs={{0,4},{4,0},{8,12},{12,8},{1,5},{5,1},{9,13},{13,9},{2,6},{6,2},{1... | collective-permute-start | bytes 393224 | tf_op jit(solution)/shard_map/ppermute | solution.py:293
  11.7 1.6 %collective-permute-start = (bf16[2,32,1024]{2,1,0:T(8,128)(2,1)}, bf16[2,32,1024]{2,1,0:T(8,128)(2,1)S(1)}, u32[]{:S(2)}, u32[]{:S(2)}) collective-permute-start(bf16[2,32,1024]{2,1,0:T(8,128)(2,1)} %spectra.1.refs_0_), channel_id=1, source_target_pairs={{0,2},{2,0},{1,3},{3,1},{4,6},{6,4},{5,7},{7,5},{8,10},{10,8},{9,1... | collective-permute-start | bytes 393224 | tf_op jit(solution)/shard_map/ppermute | solution.py:293
  13.3 0.1 reshape.63
  13.4 0.1 iota_add_fusion
  13.5 0.1 add.73
  13.6 0.1 dynamic_slice.3
  13.6 0.1 pad_add_fusion
  13.7 0.1 pad_add_fusion.1
  13.8 0.3 fusion.1
  14.1 0.3 fusion
  14.3 0.1 copy.7
  14.4 0.1 broadcast_compare_fusion
  14.5 1.1 %collective-permute-done.5.refs_3_ = bf16[2,32,1024]{2,1,0:T(8,128)(2,1)S(1)} collective-permute-done((bf16[2,32,1024]{2,1,0:T(8,128)(2,1)}, bf16[2,32,1024]{2,1,0:T(8,128)(2,1)S(1)}, u32[]{:S(2)}, u32[]{:S(2)}) %collective-permute-start.5) | collective-permute-done | bytes 131104 | tf_op jit(solution)/shard_map/ppermute | solution.py:293
  15.7 0.0 collective-permute-start.14
  15.7 0.0 collective-permute-done.11.refs_4_
  15.7 1.7 %collective-permute-start.6 = (bf16[2,32,1024]{2,1,0:T(8,128)(2,1)S(1)}, bf16[2,32,1024]{2,1,0:T(8,128)(2,1)S(1)}, u32[]{:S(2)}, u32[]{:S(2)}) collective-permute-start(bf16[2,32,1024]{2,1,0:T(8,128)(2,1)S(1)} %collective-permute-done.5.refs_3_), channel_id=1, source_target_pairs={{0,2},{2,0},{1,3},{3,1},{4,6},{6,4},{5,7},{7,5},{8,10},{10,8},{9,1... | collective-permute-start | bytes 393224 | tf_op jit(solution)/shard_map/ppermute | solution.py:293
  17.4 5.5 %collective-permute-done.3.refs_2_ = bf16[2,32,1024]{2,1,0:T(8,128)(2,1)S(1)} collective-permute-done((bf16[2,32,1024]{2,1,0:T(8,128)(2,1)}, bf16[2,32,1024]{2,1,0:T(8,128)(2,1)S(1)}, u32[]{:S(2)}, u32[]{:S(2)}) %collective-permute-start.3) | collective-permute-done | bytes 131104 | tf_op jit(solution)/shard_map/ppermute | solution.py:293
  22.9 0.0 collective-permute-start.13
  22.9 0.0 collective-permute-done.1.refs_1_
  22.9 1.5 %collective-permute-start.4 = (bf16[2,32,1024]{2,1,0:T(8,128)(2,1)S(1)}, bf16[2,32,1024]{2,1,0:T(8,128)(2,1)S(1)}, u32[]{:S(2)}, u32[]{:S(2)}) collective-permute-start(bf16[2,32,1024]{2,1,0:T(8,128)(2,1)S(1)} %collective-permute-done.3.refs_2_), channel_id=1, source_target_pairs={{0,2},{2,0},{1,3},{3,1},{4,6},{6,4},{5,7},{7,5},{8,10},{10,8},{9,1... | collective-permute-start | bytes 393224 | tf_op jit(solution)/shard_map/ppermute | solution.py:293
  24.4 0.0 collective-permute-done.refs_0_
  24.4 0.5 %collective-permute-start.2 = (bf16[2,32,1024]{2,1,0:T(8,128)(2,1)S(1)}, bf16[2,32,1024]{2,1,0:T(8,128)(2,1)S(1)}, u32[]{:S(2)}, u32[]{:S(2)}) collective-permute-start(bf16[2,32,1024]{2,1,0:T(8,128)(2,1)S(1)} %collective-permute-done.1.refs_1_), channel_id=1, source_target_pairs={{0,2},{2,0},{1,3},{3,1},{4,6},{6,4},{5,7},{7,5},{8,10},{10,8},{9,1... | collective-permute-start | bytes 393224 | tf_op jit(solution)/shard_map/ppermute | solution.py:293
  25.0 0.2 select_convert_fusion
  25.1 0.3 broadcast_in_dim.25.refs_11_
  25.5 0.0 collective-permute-done.14.refs_7_
  25.5 0.1 collective-permute-start.12
  25.5 0.0 collective-permute-done.6.refs_3_
  25.6 0.5 %collective-permute-start.7 = (bf16[2,32,1024]{2,1,0:T(8,128)(2,1)S(1)}, bf16[2,32,1024]{2,1,0:T(8,128)(2,1)S(1)}, u32[]{:S(2)}, u32[]{:S(2)}) collective-permute-start(bf16[2,32,1024]{2,1,0:T(8,128)(2,1)S(1)} %collective-permute-done.refs_0_), channel_id=1, source_target_pairs={{0,1},{1,0},{2,3},{3,2},{4,5},{5,4},{6,7},{7,6},{8,9},{9,8},{10,11... | collective-permute-start | bytes 393224 | tf_op jit(solution)/shard_map/ppermute | solution.py:293
  26.0 0.0 collective-permute-done.13.refs_6_
  26.1 0.1 collective-permute-start.10
  26.1 3.2 %collective-permute-done.4.refs_2_ = bf16[2,32,1024]{2,1,0:T(8,128)(2,1)S(1)} collective-permute-done((bf16[2,32,1024]{2,1,0:T(8,128)(2,1)S(1)}, bf16[2,32,1024]{2,1,0:T(8,128)(2,1)S(1)}, u32[]{:S(2)}, u32[]{:S(2)}) %collective-permute-start.4) | collective-permute-done | bytes 131104 | tf_op jit(solution)/shard_map/ppermute | solution.py:293
  29.3 0.0 collective-permute-start.9
  29.3 2.3 %collective-permute-done.2.refs_1_ = bf16[2,32,1024]{2,1,0:T(8,128)(2,1)S(1)} collective-permute-done((bf16[2,32,1024]{2,1,0:T(8,128)(2,1)S(1)}, bf16[2,32,1024]{2,1,0:T(8,128)(2,1)S(1)}, u32[]{:S(2)}, u32[]{:S(2)}) %collective-permute-start.2) | collective-permute-done | bytes 131104 | tf_op jit(solution)/shard_map/ppermute | solution.py:293
  31.6 0.0 collective-permute-start.8
  31.7 0.0 collective-permute-done.12.refs_5_
  31.7 0.0 copy-start
  31.7 0.9 %copy-done = bf16[2,32,1024]{2,1,0:T(8,128)(2,1)S(1)} copy-done((bf16[2,32,1024]{2,1,0:T(8,128)(2,1)S(1)}, bf16[2,32,1024]{2,1,0:T(8,128)(2,1)}, u32[]{:S(2)}) %copy-start) | copy-done | bytes 131096
  32.6 2.1 %shard_map.65.refs_9_ = f32[2,64,2,32,128]{4,3,2,1,0:T(8,128)S(1)} custom-call(bf16[2,32,1024]{2,1,0:T(8,128)(2,1)S(1)} %copy-done, bf16[2,32,1024]{2,1,0:T(8,128)(2,1)S(1)} %collective-permute-done.1.refs_1_, bf16[2,32,1024]{2,1,0:T(8,128)(2,1)S(1)} %collective-permute-done.3.refs_2_, bf16[2,32,1024]{2,1,0:T(8,128)(2,1)S(1)} %collective-permute-done.5.refs_3_, ...), custom_call_target="tpu_custom_call" | custom-call | tf_op jit(solution)/shard_map/pallas_call | solution.py:260
  34.7 0.0 copy-start.2
  34.7 2.1 %shard_map.64.refs_8_ = f32[2,64,2,32,128]{4,3,2,1,0:T(8,128)S(1)} custom-call(bf16[2,32,1024]{2,1,0:T(8,128)(2,1)S(1)} %copy-done.1, bf16[2,32,1024]{2,1,0:T(8,128)(2,1)S(1)} %collective-permute-done.1.refs_1_, bf16[2,32,1024]{2,1,0:T(8,128)(2,1)S(1)} %collective-permute-done.3.refs_2_, bf16[2,32,1024]{2,1,0:T(8,128)(2,1)S(1)} %collective-permute-done.5.refs_3_, ...), custom_call_target="tpu_custom_call" | custom-call | tf_op jit(solution)/shard_map/pallas_call | solution.py:260
  36.8 0.0 collective-permute-done.7.refs_4_
  36.8 0.0 collective-permute-done.9.refs_6_
  36.8 0.0 collective-permute-done.8.refs_5_
  36.9 8.0 %cross.1 = bf16[64,32,512]{2,1,0:T(8,128)(2,1)} custom-call(bf16[2,32,1024]{2,1,0:T(8,128)(2,1)S(1)} %collective-permute-done.refs_0_, bf16[2,32,1024]{2,1,0:T(8,128)(2,1)S(1)} %collective-permute-done.2.refs_1_, bf16[2,32,1024]{2,1,0:T(8,128)(2,1)S(1)} %collective-permute-done.4.refs_2_, bf16[2,32,1024]{2,1,0:T(8,128)(2,1)S(1)} %collective-permute-done.6.refs_3_, ...), custom_call_target="tpu_custom_call" | custom-call | tf_op jit(solution)/shard_map/cross/pallas_call | solution.py:275
  (13 shorter events, 0.0 us)
Async XLA Ops:
  0.0 13.3 %copy-start.3 = (s32[4,64]{1,0:T(4,128)S(1)}, s32[4,64]{1,0:T(4,128)}, u32[]{:S(2)}) copy-start(s32[4,64]{1,0:T(4,128)} %param.7) | copy-start | bytes 3076
  0.0 13.8 %copy-start.4 = (s32[8,128]{1,0:T(8,128)S(1)}, s32[8,128]{1,0:T(8,128)}, u32[]{:S(2)}) copy-start(s32[8,128]{1,0:T(8,128)} %param.8) | copy-start | bytes 12292
  5.9 28.8 %copy-start.1 = (bf16[2,32,1024]{2,1,0:T(8,128)(2,1)S(1)}, bf16[2,32,1024]{2,1,0:T(8,128)(2,1)}, u32[]{:S(2)}) copy-start(bf16[2,32,1024]{2,1,0:T(8,128)(2,1)} %spectra.1.refs_0_) | copy-start | bytes 393220
  5.9 9.8 %collective-permute-start.11 = (bf16[2,32,1024]{2,1,0:T(8,128)(2,1)}, bf16[2,32,1024]{2,1,0:T(8,128)(2,1)S(1)}, u32[]{:S(2)}, u32[]{:S(2)}) collective-permute-start(bf16[2,32,1024]{2,1,0:T(8,128)(2,1)} %spectra.1.refs_0_), channel_id=1, source_target_pairs={{0,1},{1,0},{2,3},{3,2},{4,5},{5,4},{6,7},{7,6},{8,9},{9,8},{10,11... | collective-permute-start | bytes 393224 | tf_op jit(solution)/shard_map/ppermute | solution.py:293
  6.4 9.3 %collective-permute-start.5 = (bf16[2,32,1024]{2,1,0:T(8,128)(2,1)}, bf16[2,32,1024]{2,1,0:T(8,128)(2,1)S(1)}, u32[]{:S(2)}, u32[]{:S(2)}) collective-permute-start(bf16[2,32,1024]{2,1,0:T(8,128)(2,1)} %spectra.1.refs_0_), channel_id=1, source_target_pairs={{0,12},{4,8},{8,4},{12,0},{1,13},{5,9},{9,5},{13,1},{2,14},{6,10},... | collective-permute-start | bytes 393224 | tf_op jit(solution)/shard_map/ppermute | solution.py:293
  11.0 11.9 %collective-permute-start.3 = (bf16[2,32,1024]{2,1,0:T(8,128)(2,1)}, bf16[2,32,1024]{2,1,0:T(8,128)(2,1)S(1)}, u32[]{:S(2)}, u32[]{:S(2)}) collective-permute-start(bf16[2,32,1024]{2,1,0:T(8,128)(2,1)} %spectra.1.refs_0_), channel_id=1, source_target_pairs={{0,8},{4,12},{8,0},{12,4},{1,9},{5,13},{9,1},{13,5},{2,10},{6,14},... | collective-permute-start | bytes 393224 | tf_op jit(solution)/shard_map/ppermute | solution.py:293
  11.0 11.9 %collective-permute-start.1 = (bf16[2,32,1024]{2,1,0:T(8,128)(2,1)}, bf16[2,32,1024]{2,1,0:T(8,128)(2,1)S(1)}, u32[]{:S(2)}, u32[]{:S(2)}) collective-permute-start(bf16[2,32,1024]{2,1,0:T(8,128)(2,1)} %spectra.1.refs_0_), channel_id=1, source_target_pairs={{0,4},{4,0},{8,12},{12,8},{1,5},{5,1},{9,13},{13,9},{2,6},{6,2},{1... | collective-permute-start | bytes 393224 | tf_op jit(solution)/shard_map/ppermute | solution.py:293
  11.7 12.8 %collective-permute-start = (bf16[2,32,1024]{2,1,0:T(8,128)(2,1)}, bf16[2,32,1024]{2,1,0:T(8,128)(2,1)S(1)}, u32[]{:S(2)}, u32[]{:S(2)}) collective-permute-start(bf16[2,32,1024]{2,1,0:T(8,128)(2,1)} %spectra.1.refs_0_), channel_id=1, source_target_pairs={{0,2},{2,0},{1,3},{3,1},{4,6},{6,4},{5,7},{7,5},{8,10},{10,8},{9,1... | collective-permute-start | bytes 393224 | tf_op jit(solution)/shard_map/ppermute | solution.py:293
  15.7 9.8 %collective-permute-start.14 = (bf16[2,32,1024]{2,1,0:T(8,128)(2,1)S(1)}, bf16[2,32,1024]{2,1,0:T(8,128)(2,1)S(1)}, u32[]{:S(2)}, u32[]{:S(2)}) collective-permute-start(bf16[2,32,1024]{2,1,0:T(8,128)(2,1)S(1)} %collective-permute-done.5.refs_3_), channel_id=1, source_target_pairs={{0,1},{1,0},{2,3},{3,2},{4,5},{5,4},{6,7},{7,6},{8,9},{9,8},{10,11... | collective-permute-start | bytes 393224 | tf_op jit(solution)/shard_map/ppermute | solution.py:293
  15.7 9.9 %collective-permute-start.6 = (bf16[2,32,1024]{2,1,0:T(8,128)(2,1)S(1)}, bf16[2,32,1024]{2,1,0:T(8,128)(2,1)S(1)}, u32[]{:S(2)}, u32[]{:S(2)}) collective-permute-start(bf16[2,32,1024]{2,1,0:T(8,128)(2,1)S(1)} %collective-permute-done.5.refs_3_), channel_id=1, source_target_pairs={{0,2},{2,0},{1,3},{3,1},{4,6},{6,4},{5,7},{7,5},{8,10},{10,8},{9,1... | collective-permute-start | bytes 393224 | tf_op jit(solution)/shard_map/ppermute | solution.py:293
  22.9 3.1 %collective-permute-start.13 = (bf16[2,32,1024]{2,1,0:T(8,128)(2,1)S(1)}, bf16[2,32,1024]{2,1,0:T(8,128)(2,1)S(1)}, u32[]{:S(2)}, u32[]{:S(2)}) collective-permute-start(bf16[2,32,1024]{2,1,0:T(8,128)(2,1)S(1)} %collective-permute-done.3.refs_2_), channel_id=1, source_target_pairs={{0,1},{1,0},{2,3},{3,2},{4,5},{5,4},{6,7},{7,6},{8,9},{9,8},{10,11... | collective-permute-start | bytes 393224 | tf_op jit(solution)/shard_map/ppermute | solution.py:293
  22.9 6.4 %collective-permute-start.4 = (bf16[2,32,1024]{2,1,0:T(8,128)(2,1)S(1)}, bf16[2,32,1024]{2,1,0:T(8,128)(2,1)S(1)}, u32[]{:S(2)}, u32[]{:S(2)}) collective-permute-start(bf16[2,32,1024]{2,1,0:T(8,128)(2,1)S(1)} %collective-permute-done.3.refs_2_), channel_id=1, source_target_pairs={{0,2},{2,0},{1,3},{3,1},{4,6},{6,4},{5,7},{7,5},{8,10},{10,8},{9,1... | collective-permute-start | bytes 393224 | tf_op jit(solution)/shard_map/ppermute | solution.py:293
  24.4 7.2 %collective-permute-start.2 = (bf16[2,32,1024]{2,1,0:T(8,128)(2,1)S(1)}, bf16[2,32,1024]{2,1,0:T(8,128)(2,1)S(1)}, u32[]{:S(2)}, u32[]{:S(2)}) collective-permute-start(bf16[2,32,1024]{2,1,0:T(8,128)(2,1)S(1)} %collective-permute-done.1.refs_1_), channel_id=1, source_target_pairs={{0,2},{2,0},{1,3},{3,1},{4,6},{6,4},{5,7},{7,5},{8,10},{10,8},{9,1... | collective-permute-start | bytes 393224 | tf_op jit(solution)/shard_map/ppermute | solution.py:293
  25.5 6.2 %collective-permute-start.12 = (bf16[2,32,1024]{2,1,0:T(8,128)(2,1)S(1)}, bf16[2,32,1024]{2,1,0:T(8,128)(2,1)S(1)}, u32[]{:S(2)}, u32[]{:S(2)}) collective-permute-start(bf16[2,32,1024]{2,1,0:T(8,128)(2,1)S(1)} %collective-permute-done.1.refs_1_), channel_id=1, source_target_pairs={{0,1},{1,0},{2,3},{3,2},{4,5},{5,4},{6,7},{7,6},{8,9},{9,8},{10,11... | collective-permute-start | bytes 393224 | tf_op jit(solution)/shard_map/ppermute | solution.py:293
  25.6 11.2 %collective-permute-start.7 = (bf16[2,32,1024]{2,1,0:T(8,128)(2,1)S(1)}, bf16[2,32,1024]{2,1,0:T(8,128)(2,1)S(1)}, u32[]{:S(2)}, u32[]{:S(2)}) collective-permute-start(bf16[2,32,1024]{2,1,0:T(8,128)(2,1)S(1)} %collective-permute-done.refs_0_), channel_id=1, source_target_pairs={{0,1},{1,0},{2,3},{3,2},{4,5},{5,4},{6,7},{7,6},{8,9},{9,8},{10,11... | collective-permute-start | bytes 393224 | tf_op jit(solution)/shard_map/ppermute | solution.py:293
  26.1 10.8 %collective-permute-start.10 = (bf16[2,32,1024]{2,1,0:T(8,128)(2,1)S(1)}, bf16[2,32,1024]{2,1,0:T(8,128)(2,1)S(1)}, u32[]{:S(2)}, u32[]{:S(2)}) collective-permute-start(bf16[2,32,1024]{2,1,0:T(8,128)(2,1)S(1)} %collective-permute-done.6.refs_3_), channel_id=1, source_target_pairs={{0,1},{1,0},{2,3},{3,2},{4,5},{5,4},{6,7},{7,6},{8,9},{9,8},{10,11... | collective-permute-start | bytes 393224 | tf_op jit(solution)/shard_map/ppermute | solution.py:293
  29.3 7.5 %collective-permute-start.9 = (bf16[2,32,1024]{2,1,0:T(8,128)(2,1)S(1)}, bf16[2,32,1024]{2,1,0:T(8,128)(2,1)S(1)}, u32[]{:S(2)}, u32[]{:S(2)}) collective-permute-start(bf16[2,32,1024]{2,1,0:T(8,128)(2,1)S(1)} %collective-permute-done.4.refs_2_), channel_id=1, source_target_pairs={{0,1},{1,0},{2,3},{3,2},{4,5},{5,4},{6,7},{7,6},{8,9},{9,8},{10,11... | collective-permute-start | bytes 393224 | tf_op jit(solution)/shard_map/ppermute | solution.py:293
  31.6 5.2 %collective-permute-start.8 = (bf16[2,32,1024]{2,1,0:T(8,128)(2,1)S(1)}, bf16[2,32,1024]{2,1,0:T(8,128)(2,1)S(1)}, u32[]{:S(2)}, u32[]{:S(2)}) collective-permute-start(bf16[2,32,1024]{2,1,0:T(8,128)(2,1)S(1)} %collective-permute-done.2.refs_1_), channel_id=1, source_target_pairs={{0,1},{1,0},{2,3},{3,2},{4,5},{5,4},{6,7},{7,6},{8,9},{9,8},{10,11... | collective-permute-start | bytes 393224 | tf_op jit(solution)/shard_map/ppermute | solution.py:293
  31.7 0.9 %copy-start = (bf16[2,32,1024]{2,1,0:T(8,128)(2,1)S(1)}, bf16[2,32,1024]{2,1,0:T(8,128)(2,1)}, u32[]{:S(2)}) copy-start(bf16[2,32,1024]{2,1,0:T(8,128)(2,1)} %spectra.1.refs_0_) | copy-start | bytes 393220
  34.7 2.2 %copy-start.2 = (bf16[1024,512]{1,0:T(8,128)(2,1)S(1)}, bf16[1024,512]{1,0:T(8,128)(2,1)}, u32[]{:S(2)}) copy-start(bf16[1024,512]{1,0:T(8,128)(2,1)} %constant.36.clone.refs_12_) | copy-start | bytes 3145732
